TPU v7x, 32 devices: a whole 2x2x4 slice. The times are simulated.
32 devices in a mesh: dom: 2 (over y), grid: 4 (over z), band: 2 (over x), mem: 2 (over core).
Axes of the slice: x: 2, y: 2, z: 4, core: 2. Of those that a mesh axis runs over, the one named last changes fastest.
Arguments:
- grid_state: bfloat16 [4, 2048, 128], P(('dom', 'mem'), 'grid'), parts along dimension 0, may hold values from -6 to 6
- forcing: bfloat16 [4096, 128], P(('dom', 'grid')), parts along dimension 0, may hold values from -6 to 6
- boundary_mask: int32 [2048], P('grid'), may hold values 0 or 1
- edge_src: int32 [4, 4, 32], P('grid'), may hold values from 0 to 511
- edge_dst: int32 [4, 4, 32], P(None, 'grid'), may hold values from 0 to 127
- edge_count: int32 [4, 4], P(None, 'grid'), may hold values from 0 to 32, as said below
- edge_weight: float32 [4, 4, 32], P(None, 'grid'), may hold values from 0.1 to 1
- embed_weight: bfloat16 [128, 1024], P(None, 'band'), may hold values from -0.5 to 0.5
- attn_qkv: bfloat16 [1, 1024, 3, 1024], P(None, 'mem', None, 'band'), may hold values from -0.1875 to 0.1875
- attn_out: bfloat16 [1, 1024, 1024], P(None, 'band', 'mem'), may hold values from -0.1875 to 0.1875
- mlp_in: bfloat16 [1, 1024, 4096], P(None, 'mem', 'band'), may hold values from -0.1875 to 0.1875
- mlp_out: bfloat16 [1, 4096, 1024], P(None, 'band', 'mem'), may hold values from -0.09375 to 0.09375
- decode_weight: bfloat16 [1024, 128], P('band'), may hold values from -0.1875 to 0.1875
Outputs:
- next_state: bfloat16 [4, 2048, 128], P(('dom', 'mem'), 'grid'), parts along dimension 0
There are 2 independent parts, one for each index of `dom`. A program takes and returns all parts, laid end to end along the dimension named above; an argument that names none is the same for every part. Nothing has to cross between parts.
Inputs may be any that keep to these rules, and one draw needn't show every extreme that they name: Slots at or beyond edge_count[i, j] in a block are padding. In every draw some mesh band receives 32 live slots from every grid shard.
All inputs are finite; a program needn't handle non-finite values. No bound on the sum of `boundary_mask` on one device may be relied on, other than what follows from the above.
Results may differ from a plain program's by a relative error of at most 0.011.
Values may be sent and summed in bfloat16 or wider, within the bound.
No kernel may reach another device: no remote copies, remote signals or barrier semaphores. Data moves between devices by JAX's collectives and lax.ppermute only.
A program may use at most 64 MiB of HBM per device.

v0:
```python
import jax
import jax.numpy as jnp
from jax import lax
from jax.sharding import PartitionSpec as P

HEADS = 16
GP_DEV = 512
M_DEV = 128
WINDOW = 64


def extended(block, sides, width):
    for axis, dim in sides:
        count = lax.axis_size(axis)
        forward = [(i, i + 1) for i in range(count - 1)]
        backward = [(target, source) for source, target in forward]
        low = lax.ppermute(
            lax.slice_in_dim(block, block.shape[dim] - width, None, axis=dim), axis, forward
        )
        high = lax.ppermute(lax.slice_in_dim(block, 0, width, axis=dim), axis, backward)
        block = jnp.concatenate([low, block, high], axis=dim)
    return block


def rms_norm(values):
    return values * lax.rsqrt(jnp.mean(values * values, axis=-1, keepdims=True) + 1e-06)


def body(
    grid_state,
    forcing,
    boundary_mask,
    edge_src,
    edge_dst,
    edge_count,
    edge_weight,
    embed_weight,
    attn_qkv,
    attn_out,
    mlp_in,
    mlp_out,
    decode_weight,
):
    shards = lax.axis_size("grid")
    grid_index = lax.axis_index("grid")
    col_width = embed_weight.shape[1]
    grid_rows = grid_state[0]
    var_count = grid_rows.shape[1]
    slot_count = edge_dst.shape[2]
    sources = edge_src[0].reshape(-1)
    targets = edge_dst[:, 0].reshape(-1)
    live_slot = jnp.arange(slot_count, dtype=jnp.int32)[None, :] < edge_count[:, 0][:, None]
    weights = jnp.where(live_slot, edge_weight[:, 0], 0.0).reshape(-1)
    embedded = jax.nn.gelu(jnp.dot(grid_rows, embed_weight, preferred_element_type=jnp.float32))
    picked = embedded[sources].reshape(shards, slot_count, col_width)
    arrived = lax.all_to_all(
        picked.astype(jnp.bfloat16), "grid", split_axis=0, concat_axis=0, tiled=True
    ).astype(picked.dtype)
    latent = arrived.reshape(-1, col_width)
    mesh_part = jax.ops.segment_sum(latent * weights[:, None], targets, num_segments=M_DEV)
    mesh_in = lax.all_gather(mesh_part.astype(jnp.bfloat16), "band", axis=1, tiled=True)
    stream = mesh_in.astype(jnp.float32)
    mesh_rows = stream.shape[0]
    model_width = stream.shape[1]
    head_dim = model_width // HEADS
    local_heads = col_width // head_dim
    query_pos = grid_index * mesh_rows + jnp.arange(mesh_rows, dtype=jnp.int32)
    key_pos = grid_index * mesh_rows - WINDOW + jnp.arange(mesh_rows + 2 * WINDOW, dtype=jnp.int32)
    visible = (
        (jnp.abs(query_pos[:, None] - key_pos[None, :]) <= WINDOW)
        & (key_pos[None, :] >= 0)
        & (key_pos[None, :] < mesh_rows * shards)
    )
    w_qkv = lax.all_gather(attn_qkv[0], "mem", axis=0, tiled=True)
    w_out = lax.all_gather(attn_out[0], "mem", axis=1, tiled=True)
    w_in = lax.all_gather(mlp_in[0], "mem", axis=0, tiled=True)
    w_back = lax.all_gather(mlp_out[0], "mem", axis=1, tiled=True)
    normed = rms_norm(stream).astype(jnp.bfloat16)
    mixed_qkv = jnp.dot(
        normed, w_qkv.reshape(model_width, 3 * col_width), preferred_element_type=jnp.float32
    )
    mixed_qkv = mixed_qkv.reshape(mesh_rows, 3, local_heads, head_dim)
    queries = rms_norm(mixed_qkv[:, 0]).astype(jnp.bfloat16)
    keys_now = rms_norm(mixed_qkv[:, 1]).astype(jnp.bfloat16).reshape(mesh_rows, col_width)
    values = mixed_qkv[:, 2].astype(jnp.bfloat16).reshape(mesh_rows, col_width)
    padded = extended(jnp.stack([keys_now, values]), (("grid", 1),), WINDOW)
    near_keys = padded[0].reshape(-1, local_heads, head_dim)
    near_values = padded[1].reshape(-1, local_heads, head_dim)
    scores = jnp.einsum(
        "qhd,khd->hqk", queries, near_keys, preferred_element_type=jnp.float32
    ) * head_dim ** (-0.5)
    exp_scores = jnp.where(visible[None], jnp.exp(scores), 0.0)
    shares = (exp_scores / jnp.sum(exp_scores, axis=-1, keepdims=True)).astype(jnp.bfloat16)
    attended = jnp.einsum("hqk,khd->qhd", shares, near_values, preferred_element_type=jnp.float32)
    attended = attended.astype(jnp.bfloat16).reshape(mesh_rows, col_width)
    stream = stream + lax.psum(
        jnp.dot(attended, w_out, preferred_element_type=jnp.float32).astype(jnp.bfloat16), "band"
    ).astype(jnp.float32)
    normed = rms_norm(stream).astype(jnp.bfloat16)
    hidden = jax.nn.gelu(jnp.dot(normed, w_in, preferred_element_type=jnp.float32)).astype(
        jnp.bfloat16
    )
    stream = stream + lax.psum(
        jnp.dot(hidden, w_back, preferred_element_type=jnp.float32).astype(jnp.bfloat16), "band"
    ).astype(jnp.float32)
    mesh_out = stream.astype(jnp.bfloat16)
    mesh_cols = lax.dynamic_slice_in_dim(mesh_out, lax.axis_index("band") * col_width, col_width, 1)
    projected = lax.psum(
        jnp.dot(mesh_cols, decode_weight, preferred_element_type=jnp.float32).astype(jnp.bfloat16),
        "band",
    ).astype(jnp.float32)
    outgoing = (projected[targets] * weights[:, None]).reshape(shards, slot_count, var_count)
    returned = lax.all_to_all(
        outgoing.astype(jnp.bfloat16), "grid", split_axis=0, concat_axis=0, tiled=True
    ).astype(outgoing.dtype)
    decoded = jax.ops.segment_sum(returned.reshape(-1, var_count), sources, num_segments=GP_DEV)
    forced = boundary_mask[:, None] == 1
    result = jnp.where(forced, forcing.astype(jnp.float32), grid_rows.astype(jnp.float32) + decoded)
    return result.astype(jnp.bfloat16)[None]


def solution(mesh):
    return jax.shard_map(
        body,
        mesh=mesh,
        in_specs=(
            P(("dom", "mem"), "grid", None),
            P(("dom", "grid"), None),
            P("grid"),
            P("grid", None, None),
            P(None, "grid", None),
            P(None, "grid"),
            P(None, "grid", None),
            P(None, "band"),
            P(None, "mem", None, "band"),
            P(None, "band", "mem"),
            P(None, "mem", "band"),
            P(None, "band", "mem"),
            P("band", None),
        ),
        out_specs=P(("dom", "mem"), "grid", None),
        check_vma=False,
    )
```

profile of v0, /device:TPU:0, one launch (start us, length us, event | category | flops | bytes accessed | tf_op | source)
XLA Modules:
  0.0 162.2 jit_solution(17599511599854920596)
XLA Ops:
  6.6 2.7 %copy.14 = bf16[1,512,3,512]{1,3,2,0:T(8,128)(2,1)} copy(bf16[1,512,3,512]{3,1,2,0:T(8,128)(2,1)} %param.21) | data formatting | bytes 3145728 | tf_op args[8]
  10.0 1.5 gather_fusion
  11.5 6.3 %all-to-all-start = ((bf16[4,32,512]{2,1,0:T(8,128)(2,1)}), bf16[4,32,512]{2,1,0:T(8,128)(2,1)S(1)}, u32[]{:S(2)}, u32[]{:S(2)}) async-start(bf16[4,32,512]{2,1,0:T(8,128)(2,1)} %bitcast.2), calls=%async_computation | async-start | bytes 262144 | tf_op jit(solution)/shard_map/all_to_all | solution.py:56
  21.3 2.6 %all-to-all-done = bf16[4,32,512]{2,1,0:T(8,128)(2,1)S(1)} async-done(((bf16[4,32,512]{2,1,0:T(8,128)(2,1)}), bf16[4,32,512]{2,1,0:T(8,128)(2,1)S(1)}, u32[]{:S(2)}, u32[]{:S(2)}) %all-to-all-start) | async-done | bytes 131104 | tf_op jit(solution)/shard_map/all_to_all | solution.py:56
  23.9 1.5 scatter_custom_fusion
  25.4 5.6 %all_gather.15 = bf16[128,1024]{1,0:T(8,128)(2,1)S(1)} all-gather(bf16[128,512]{1,0:T(8,128)(2,1)S(1)} %convert_element_type.93), channel_id=1, replica_groups=mesh['dom'=2,'grid'=4,'band'=2,'mem'=2] {'band'}, dimensions={1}, use_global_device_ids=true | all-gather | bytes 393216 | tf_op jit(solution)/shard_map/all_gather | solution.py:61
  31.2 3.0 %fusion.39 = f32[128,3,8,64]{0,3,2,1:T(8,128)S(1)} fusion(bf16[3,8,64,1024]{3,2,1,0:T(8,128)(2,1)} %bitcast.72, bf16[128,1024]{1,0:T(8,128)(2,1)S(1)} %all_gather.15, f32[128]{0:T(128)S(1)} %add_rsqrt_fusion.3), kind=kOutput, calls=%fused_computation.48 | convolution fusion | flops 403046400 | bytes 4194816 | tf_op jit(solution)/shard_map/dot_general | solution.py:79
  34.5 3.0 %collective-permute-start = (bf16[2,64,512]{1,2,0:T(8,128)(2,1)S(1)}, bf16[2,64,512]{1,2,0:T(8,128)(2,1)S(1)}, u32[]{:S(2)}, u32[]{:S(2)}) collective-permute-start(bf16[2,64,512]{1,2,0:T(8,128)(2,1)S(1)} %get-tuple-element.11), channel_id=1, source_target_pairs={{0,4},{4,8},{8,12},{1,5},{5,9},{9,13},{2,6},{6,10},{10,14},{3,7},{... | collective-permute-start | bytes 393224 | tf_op jit(solution)/shard_map/ppermute | solution.py:17
  37.5 1.3 collective-permute-start.1
  38.8 2.5 %collective-permute-done = bf16[2,64,512]{1,2,0:T(8,128)(2,1)S(1)} collective-permute-done((bf16[2,64,512]{1,2,0:T(8,128)(2,1)S(1)}, bf16[2,64,512]{1,2,0:T(8,128)(2,1)S(1)}, u32[]{:S(2)}, u32[]{:S(2)}) %collective-permute-start) | collective-permute-done | bytes 131104 | tf_op jit(solution)/shard_map/ppermute | solution.py:17
  41.3 4.4 %collective-permute-done.1 = bf16[2,64,512]{1,2,0:T(8,128)(2,1)S(1)} collective-permute-done((bf16[2,64,512]{1,2,0:T(8,128)(2,1)S(1)}, bf16[2,64,512]{1,2,0:T(8,128)(2,1)S(1)}, u32[]{:S(2)}, u32[]{:S(2)}) %collective-permute-start.1) | collective-permute-done | bytes 131104 | tf_op jit(solution)/shard_map/ppermute | solution.py:20
  46.9 2.3 %convolution_convert_fusion = bf16[128,1024]{1,0:T(8,128)(2,1)} fusion(bf16[128,512]{0,1:T(8,128)(2,1)S(1)} %bitcast.80, bf16[1,512,1024]{2,1,0:T(8,128)(2,1)} %all-gather.11.cloned.1.call-done), kind=kOutput, calls=%fused_computation.13 | convolution fusion | flops 134348800 | bytes 1441792 | tf_op jit(solution)/shard_map/dot_general | solution.py:97
  50.6 20.6 %all-reduce.3.cloned.1.call-done = bf16[128,1024]{1,0:T(8,128)(2,1)} async-done(((bf16[128,1024]{1,0:T(8,128)(2,1)}), bf16[128,1024]{1,0:T(8,128)(2,1)}) %all-reduce.3.cloned.1.call-update) | async-done | bytes 262160 | tf_op jit(solution)/shard_map/psum | solution.py:96
  71.2 1.1 multiply_reduce_fusion
  72.4 13.9 %all-gather.13.cloned.1.call-done = bf16[1,1024,2048]{2,1,0:T(8,128)(2,1)} async-done(((bf16[1,512,2048]{2,1,0:T(8,128)(2,1)}), bf16[1,1024,2048]{2,1,0:T(8,128)(2,1)}) %all-gather.13.cloned.1.call-update) | async-done | bytes 4194320 | tf_op jit(solution)/shard_map/all_gather | solution.py:76
  86.3 16.3 %all-gather.15.cloned.1.call-done = bf16[1,2048,1024]{2,1,0:T(8,128)(2,1)} async-done(((bf16[1,2048,512]{2,1,0:T(8,128)(2,1)}), bf16[1,2048,1024]{2,1,0:T(8,128)(2,1)}) %all-gather.15.cloned.1.call-update) | async-done | bytes 4194320 | tf_op jit(solution)/shard_map/all_gather | solution.py:77
  102.6 5.9 %fusion.6 = bf16[128,1024]{1,0:T(8,128)(2,1)} fusion(bf16[1,2048,1024]{2,1,0:T(8,128)(2,1)} %all-gather.15.cloned.1.call-done, bf16[1,1024,2048]{2,1,0:T(8,128)(2,1)} %all-gather.13.cloned.1.call-done, f32[128]{0:T(128)S(1)} %add_rsqrt_fusion.2, bf16[128,1024]{1,0:T(8,128)(2,1)S(1)} %all_gather.15, bf16[128,1024]{1,0:T(8,128)(2,1)} %all-reduce.3.cloned.1.call-done), kind=kOutput, calls=%fused_computation.14 | convolution fusion | flops 1076887552 | bytes 9175552 | tf_op jit(solution)/shard_map/dot_general | solution.py:104
  108.5 24.5 %all-reduce.5.cloned.1.call-done = bf16[128,1024]{1,0:T(8,128)(2,1)} async-done(((bf16[128,1024]{1,0:T(8,128)(2,1)}), bf16[128,1024]{1,0:T(8,128)(2,1)}) %all-reduce.5.cloned.1.call-update) | async-done | bytes 262160 | tf_op jit(solution)/shard_map/psum | solution.py:103
  133.1 1.1 convolution_convert_fusion.2
  134.2 7.1 %psum.23 = bf16[128,128]{1,0:T(8,128)(2,1)S(1)} all-reduce(bf16[128,128]{1,0:T(8,128)(2,1)S(1)} %convolution_convert_fusion.2), channel_id=1, replica_groups=mesh['dom'=2,'grid'=4,'band'=2,'mem'=2] {'band'}, use_global_device_ids=true, to_apply=%region_8.9 | all-reduce | flops 16384 | bytes 65536 | tf_op jit(solution)/shard_map/psum | solution.py:108
  142.7 4.9 %all-to-all-start.1 = ((bf16[4,32,128]{2,1,0:T(8,128)(2,1)}), bf16[4,32,128]{2,1,0:T(8,128)(2,1)S(1)}, u32[]{:S(2)}, u32[]{:S(2)}) async-start(bf16[4,32,128]{2,1,0:T(8,128)(2,1)} %multiply_convert_fusion.5), calls=%async_computation.1 | async-start | bytes 65536 | tf_op jit(solution)/shard_map/all_to_all | solution.py:113
  147.6 5.6 %all-to-all-done.1 = bf16[4,32,128]{2,1,0:T(8,128)(2,1)S(1)} async-done(((bf16[4,32,128]{2,1,0:T(8,128)(2,1)}), bf16[4,32,128]{2,1,0:T(8,128)(2,1)S(1)}, u32[]{:S(2)}, u32[]{:S(2)}) %all-to-all-start.1) | async-done | bytes 32800 | tf_op jit(solution)/shard_map/all_to_all | solution.py:113
  153.2 1.4 scatter_custom_fusion.1
  154.6 0.8 fusion.47
  (74 shorter events, 8.5 us)
Async XLA Ops:
  6.5 2.9 %copy-start = (bf16[128,512]{1,0:T(8,128)(2,1)S(1)}, bf16[128,512]{1,0:T(8,128)(2,1)}, u32[]{:S(2)}) copy-start(bf16[128,512]{1,0:T(8,128)(2,1)} %param.20) | copy-start | bytes 393220
  6.5 2.8 %copy-start.4 = (s32[1,4,32]{2,1,0:T(4,128)S(1)}, s32[1,4,32]{2,1,0:T(4,128)}, u32[]{:S(2)}) copy-start(s32[1,4,32]{2,1,0:T(4,128)} %param.16) | copy-start | bytes 1540
  6.5 2.9 %copy-start.1 = (bf16[1,512,128]{2,1,0:T(8,128)(2,1)S(1)}, bf16[1,512,128]{2,1,0:T(8,128)(2,1)}, u32[]{:S(2)}) copy-start(bf16[1,512,128]{2,1,0:T(8,128)(2,1)} %param.13) | copy-start | bytes 393220
  6.5 12.1 %copy-start.8 = (s32[4,1]{0,1:T(1,128)S(1)}, s32[4,1]{0,1:T(1,128)}, u32[]{:S(2)}) copy-start(s32[4,1]{0,1:T(1,128)} %param.18) | copy-start | bytes 52
  6.5 12.8 %copy-start.6 = (f32[4,1,32]{2,1,0:T(1,128)S(1)}, f32[4,1,32]{2,1,0:T(1,128)}, u32[]{:S(2)}) copy-start(f32[4,1,32]{2,1,0:T(1,128)} %param.19) | copy-start | bytes 1540
  6.5 13.9 %copy-start.5 = (s32[4,1,32]{2,1,0:T(1,128)S(1)}, s32[4,1,32]{2,1,0:T(1,128)}, u32[]{:S(2)}) copy-start(s32[4,1,32]{2,1,0:T(1,128)} %param.17) | copy-start | bytes 1540
  6.6 24.6 %all-gather.9.cloned.1.call-start = ((), (), s32[]{:S(2)}) async-start(), calls=%async_computation.4 | async-start | bytes 4718592 | tf_op jit(solution)/shard_map/all_gather | solution.py:74
  11.5 12.4 %all-to-all-start = ((bf16[4,32,512]{2,1,0:T(8,128)(2,1)}), bf16[4,32,512]{2,1,0:T(8,128)(2,1)S(1)}, u32[]{:S(2)}, u32[]{:S(2)}) async-start(bf16[4,32,512]{2,1,0:T(8,128)(2,1)} %bitcast.2), calls=%async_computation | async-start | bytes 262144 | tf_op jit(solution)/shard_map/all_to_all | solution.py:56
  17.8 29.1 %all-gather.11.cloned.1.call-start = ((), (), s32[]{:S(2)}) async-start(), calls=%async_computation.5 | async-start | bytes 1572864 | tf_op jit(solution)/shard_map/all_gather | solution.py:75
  18.5 52.7 %all-reduce.3.cloned.1.call-start = ((), (), s32[]{:S(2)}) async-start(), calls=%async_computation.2 | async-start | bytes 524288 | tf_op jit(solution)/shard_map/psum | solution.py:96
  34.5 6.9 %collective-permute-start = (bf16[2,64,512]{1,2,0:T(8,128)(2,1)S(1)}, bf16[2,64,512]{1,2,0:T(8,128)(2,1)S(1)}, u32[]{:S(2)}, u32[]{:S(2)}) collective-permute-start(bf16[2,64,512]{1,2,0:T(8,128)(2,1)S(1)} %get-tuple-element.11), channel_id=1, source_target_pairs={{0,4},{4,8},{8,12},{1,5},{5,9},{9,13},{2,6},{6,10},{10,14},{3,7},{... | collective-permute-start | bytes 393224 | tf_op jit(solution)/shard_map/ppermute | solution.py:17
  37.5 8.3 %collective-permute-start.1 = (bf16[2,64,512]{1,2,0:T(8,128)(2,1)S(1)}, bf16[2,64,512]{1,2,0:T(8,128)(2,1)S(1)}, u32[]{:S(2)}, u32[]{:S(2)}) collective-permute-start(bf16[2,64,512]{1,2,0:T(8,128)(2,1)S(1)} %get-tuple-element.12), channel_id=1, source_target_pairs={{4,0},{8,4},{12,8},{5,1},{9,5},{13,9},{6,2},{10,6},{14,10},{7,3},{... | collective-permute-start | bytes 393224 | tf_op jit(solution)/shard_map/ppermute | solution.py:20
  49.2 37.1 %all-gather.13.cloned.1.call-start = ((), (), s32[]{:S(2)}) async-start(), calls=%async_computation.6 | async-start | bytes 6291456 | tf_op jit(solution)/shard_map/all_gather | solution.py:76
  49.8 52.8 %all-gather.15.cloned.1.call-start = ((), (), s32[]{:S(2)}) async-start(), calls=%async_computation.7 | async-start | bytes 6291456 | tf_op jit(solution)/shard_map/all_gather | solution.py:77
  50.4 82.7 %all-reduce.5.cloned.1.call-start = ((), (), s32[]{:S(2)}) async-start(), calls=%async_computation.3 | async-start | bytes 524288 | tf_op jit(solution)/shard_map/psum | solution.py:103
  72.3 60.7 %copy-start.2 = (bf16[512,128]{1,0:T(8,128)(2,1)S(1)}, bf16[512,128]{1,0:T(8,128)(2,1)}, u32[]{:S(2)}) copy-start(bf16[512,128]{1,0:T(8,128)(2,1)} %param.25) | copy-start | bytes 393220
  72.4 75.2 %copy-start.7 = (s32[512]{0:T(512)S(1)}, s32[512]{0:T(512)}, u32[]{:S(2)}) copy-start(s32[512]{0:T(512)} %param.15) | copy-start | bytes 6148
  72.4 82.2 %copy-start.3 = (bf16[512,128]{1,0:T(8,128)(2,1)S(1)}, bf16[512,128]{1,0:T(8,128)(2,1)}, u32[]{:S(2)}) copy-start(bf16[512,128]{1,0:T(8,128)(2,1)} %param.14) | copy-start | bytes 393220
  142.7 10.5 %all-to-all-start.1 = ((bf16[4,32,128]{2,1,0:T(8,128)(2,1)}), bf16[4,32,128]{2,1,0:T(8,128)(2,1)S(1)}, u32[]{:S(2)}, u32[]{:S(2)}) async-start(bf16[4,32,128]{2,1,0:T(8,128)(2,1)} %multiply_convert_fusion.5), calls=%async_computation.1 | async-start | bytes 65536 | tf_op jit(solution)/shard_map/all_to_all | solution.py:113
Sparse Core Ops, SparseCore 0:
  9.5 14.8 all-gather.8
  25.9 10.1 all-gather.10
  49.4 21.8 all-reduce.2
  72.6 13.6 all-gather.12
  87.7 14.8 all-gather.14
  108.6 24.4 all-reduce.4
where the time goes:
time: 163 us; the launch traced here: 162 us
  waiting for transfers between devices  92.3 us (57%)
  starting transfers between devices  15.7 us (10%)
  between operations  13.8 us (8%)
  matrix products  13.5 us (8%)
  blocking collectives  12.8 us (8%)
  other arithmetic  7.68 us (5%)
  local copies, waits for them, and re-layouts  6.48 us (4%)
    psum x1, waiting for transfers between devices, body(): lax.psum(jnp.dot(hidden, w_back, preferred_element_type=jnp.float32).asty...  24.5 us
    psum x1, waiting for transfers between devices, body(): lax.psum(jnp.dot(attended, w_out, preferred_element_type=jnp.float32).ast...  20.6 us
    all_gather x1, waiting for transfers between devices, body(): w_back = lax.all_gather(mlp_out[0], 'mem', axis=1, tiled=True)  16.3 us
    all_gather x1, waiting for transfers between devices, body(): w_in = lax.all_gather(mlp_in[0], 'mem', axis=0, tiled=True)  13.9 us
    psum x1, blocking collectives, body(): lax.psum(jnp.dot(mesh_cols, decode_weight, preferred_element_type=jnp.flo...  7.13 us
    all_to_all x1, starting transfers between devices, body(): lax.all_to_all(picked.astype(jnp.bfloat16), 'grid', split_axis=0, concat_...  6.34 us
    dot_general x1, matrix products, body(): jnp.dot(hidden, w_back, preferred_element_type=jnp.float32)  5.88 us
    all_gather x1, blocking collectives, body(): lax.all_gather(mesh_part.astype(jnp.bfloat16), 'band', axis=1, tiled=True)  5.64 us
  transfers between devices with their start and end apart: 10, of which 8 were waited for; matrix products, arithmetic and copies ran while one was open for 7% of the time, Pallas kernels for 0%

commit v1 on v0

v1 whole, which is shorter than its diff:
```python
import jax
import jax.numpy as jnp
from jax import lax
from jax.sharding import PartitionSpec as P

HEADS = 16
M_DEV = 128
WINDOW = 64
DIRECT_PEERS = 8
BF16 = jnp.bfloat16
F32 = jnp.float32


def matmul(left, right):
    return jnp.dot(left, right, preferred_element_type=F32)


def shifted(block, axes, offsets):
    sizes = [lax.axis_size(axis) for axis in axes]
    pairs = []
    total = 1
    for size in sizes:
        total *= size
    for source in range(total):
        rest, coords = source, []
        for size in reversed(sizes):
            coords.append(rest % size)
            rest //= size
        coords.reverse()
        target = 0
        for coord, offset, size in zip(coords, offsets, sizes):
            target = target * size + (coord + offset) % size
        pairs.append((source, target))
    return lax.ppermute(block, tuple(axes), pairs)


def ring(block, axis):
    count = lax.axis_size(axis)
    return [block] + [shifted(block, (axis,), (step,)) for step in range(1, count)]


def choose(options, index):
    picked = options[0]
    for at in range(1, len(options)):
        picked = jnp.where(index == at, options[at], picked)
    return picked


def rms_norm(values):
    return values * lax.rsqrt(jnp.mean(values * values, axis=-1, keepdims=True) + 1e-06)


def hi_lo(values):
    high = values.astype(BF16)
    return high, (values - high.astype(F32)).astype(BF16)


def body(
    grid_state,
    forcing,
    boundary_mask,
    edge_src,
    edge_dst,
    edge_count,
    edge_weight,
    embed_weight,
    attn_qkv,
    attn_out,
    mlp_in,
    mlp_out,
    decode_weight,
):
    shards, bands, mems = (lax.axis_size(axis) for axis in ("grid", "band", "mem"))
    grid_at, band_at, mem_at = (lax.axis_index(axis) for axis in ("grid", "band", "mem"))
    direct = shards * bands <= DIRECT_PEERS
    rows = grid_state[0]
    points, channels = rows.shape
    slots = edge_dst.shape[2]
    model_half = attn_qkv.shape[1]
    col_width = attn_qkv.shape[3]
    head_dim = model_half * mems // HEADS
    heads = col_width // head_dim
    pieces = bands // mems

    def mem_order(block, dim):
        got = ring(block, "band")
        parts = []
        for step in range(mems):
            for inner in range(pieces):
                shard = ((mem_at - step) % mems) * pieces + inner
                parts.append(choose(got, (band_at - shard) % bands))
        return jnp.concatenate(parts, axis=dim)

    def by_arrival(values):
        if not direct:
            return values
        back = values[::-1]
        return lax.dynamic_slice_in_dim(
            jnp.concatenate([back, back]), shards - 1 - grid_at, shards, 0
        )

    targets = edge_dst[:, 0]
    live = jnp.arange(slots, dtype=jnp.int32)[None, :] < edge_count[:, 0][:, None]
    weights = jnp.where(live, edge_weight[:, 0], 0.0)
    sources = jnp.pad(edge_src[0], ((1, 1), (0, 0)))
    if direct:
        towards = [(grid_at + step) % shards for step in range(shards)]
    else:
        towards = list(range(shards))
    wanted = jnp.concatenate(
        [lax.dynamic_slice_in_dim(sources, at, 3, 0).reshape(-1) for at in towards]
    )
    spread = (wanted[:, None] == jnp.arange(points, dtype=jnp.int32)[None, :]).astype(BF16)
    picked = matmul(spread, rows).astype(BF16).reshape(shards, 3 * slots, channels)
    weight_high, weight_low = hi_lo(weights)
    info = jnp.stack([targets.astype(BF16), weight_high, weight_low]).reshape(-1)
    info_rows = -(-info.size // (16 * channels)) * 16
    info = jnp.pad(info, (0, info_rows * channels - info.size)).reshape(info_rows, channels)
    if direct:
        arrived = [picked[0]]
        notes = {}
        for step in range(1, shards):
            if step in (1, shards - 1):
                message = shifted(jnp.concatenate([picked[step], info]), ("grid",), (step,))
                notes[step] = message[3 * slots :]
                arrived.append(message[: 3 * slots])
            else:
                arrived.append(shifted(picked[step], ("grid",), (step,)))
        arrived = jnp.concatenate(arrived)
        below, above = notes[1], notes[shards - 1]
    else:
        message = jnp.concatenate(
            [picked, jnp.broadcast_to(info[None], (shards,) + info.shape)], axis=1
        )
        message = lax.all_to_all(message, "grid", 0, 0, tiled=True)
        arrived = message[:, : 3 * slots].reshape(-1, channels)
        below = message[(grid_at - 1) % shards, 3 * slots :]
        above = message[(grid_at + 1) % shards, 3 * slots :]

    def unpack(note, inside):
        note = note.reshape(-1)[: 3 * shards * slots].reshape(3, shards, slots).astype(F32)
        return note[0].astype(jnp.int32), jnp.where(inside, note[1] + note[2], 0.0)

    embed_full = mem_order(embed_weight, 1)
    qkv_parts = ring(attn_qkv[0], "mem")
    out_parts = ring(attn_out[0], "mem")
    in_parts = ring(mlp_in[0], "mem")
    decode_full = mem_order(decode_weight, 0)
    folded = ring(matmul(mlp_out[0], decode_full[:model_half]), "mem")
    folded = sum(folded[1:], folded[0]).astype(BF16)

    below_dst, below_weight = unpack(below, grid_at > 0)
    above_dst, above_weight = unpack(above, grid_at < shards - 1)
    places = jnp.stack([below_dst - M_DEV, targets, above_dst + M_DEV], axis=1) + WINDOW
    place_weights = jnp.stack([below_weight, weights, above_weight], axis=1)
    places = by_arrival(places).reshape(-1)
    place_weights = by_arrival(place_weights).reshape(-1)
    extent = M_DEV + 2 * WINDOW
    collect = jnp.where(
        jnp.arange(extent, dtype=jnp.int32)[:, None] == places[None, :], place_weights[None, :], 0.0
    )
    collect_high, collect_low = hi_lo(collect)
    embedded = jax.nn.gelu(matmul(arrived, embed_full)).astype(BF16)
    mesh_in = (matmul(collect_high, embedded) + matmul(collect_low, embedded)).astype(BF16)
    wide_stream = mesh_in.astype(F32)

    normed = rms_norm(wide_stream).astype(BF16)
    mixed = sum(
        matmul(
            normed[:, step * model_half : (step + 1) * model_half],
            part.reshape(model_half, 3 * col_width),
        )
        for step, part in enumerate(qkv_parts)
    ).reshape(extent, 3, heads, head_dim)
    queries = rms_norm(mixed[WINDOW : WINDOW + M_DEV, 0]).astype(BF16)
    keys = rms_norm(mixed[:, 1]).astype(BF16)
    values = mixed[:, 2].astype(BF16)
    query_pos = grid_at * M_DEV + jnp.arange(M_DEV, dtype=jnp.int32)
    key_pos = grid_at * M_DEV - WINDOW + jnp.arange(extent, dtype=jnp.int32)
    visible = (
        (jnp.abs(query_pos[:, None] - key_pos[None, :]) <= WINDOW)
        & (key_pos[None, :] >= 0)
        & (key_pos[None, :] < M_DEV * shards)
    )
    scores = jnp.einsum("qhd,khd->hqk", queries, keys, preferred_element_type=F32) * head_dim ** (
        -0.5
    )
    exp_scores = jnp.where(visible[None], jnp.exp(scores), 0.0)
    shares = (exp_scores / jnp.sum(exp_scores, axis=-1, keepdims=True)).astype(BF16)
    attended = jnp.einsum("hqk,khd->qhd", shares, values, preferred_element_type=F32)
    attended = attended.astype(BF16).reshape(M_DEV, col_width)
    product = jnp.concatenate([matmul(attended, part) for part in out_parts], axis=1).astype(BF16)
    products = ring(product, "band")
    stream = wide_stream[WINDOW : WINDOW + M_DEV]
    stream = stream + sum(part.astype(F32) for part in products)

    normed = rms_norm(stream).astype(BF16)
    hidden = jax.nn.gelu(
        sum(
            matmul(normed[:, step * model_half : (step + 1) * model_half], part)
            for step, part in enumerate(in_parts)
        )
    ).astype(BF16)
    carried = jnp.where(band_at == 0, stream, 0.0).astype(BF16)
    projected = (matmul(hidden, folded) + matmul(carried, decode_full)).astype(BF16)
    reach = (
        targets.reshape(-1)[:, None] == jnp.arange(M_DEV, dtype=jnp.int32)[None, :]
    ).astype(BF16)
    outgoing = (matmul(reach, projected) * weights.reshape(-1)[:, None]).astype(BF16)
    outgoing = outgoing.reshape(shards, slots, channels)
    if direct:
        returned = []
        for band_step in range(bands):
            for step in range(shards):
                block = lax.dynamic_index_in_dim(
                    outgoing, (grid_at + step) % shards, 0, keepdims=False
                )
                if step or band_step:
                    block = shifted(block, ("grid", "band"), (step, band_step))
                returned.append(block)
        returned = jnp.concatenate(returned)
        copies = bands
    else:
        summed = sum(part.astype(F32) for part in ring(outgoing, "band"))
        returned = lax.all_to_all(summed.astype(BF16), "grid", 0, 0, tiled=True)
        returned = returned.reshape(-1, channels)
        copies = 1
    home = by_arrival(edge_src[0]).reshape(-1)
    scatter = (jnp.arange(points, dtype=jnp.int32)[:, None] == home[None, :]).astype(BF16)
    decoded = matmul(jnp.concatenate([scatter] * copies, axis=1), returned)
    forced = boundary_mask[:, None] == 1
    result = jnp.where(forced, forcing.astype(F32), rows.astype(F32) + decoded)
    return result.astype(BF16)[None]


def solution(mesh):
    return jax.shard_map(
        body,
        mesh=mesh,
        in_specs=(
            P(("dom", "mem"), "grid", None),
            P(("dom", "grid"), None),
            P("grid"),
            P("grid", None, None),
            P(None, "grid", None),
            P(None, "grid"),
            P(None, "grid", None),
            P(None, "band"),
            P(None, "mem", None, "band"),
            P(None, "band", "mem"),
            P(None, "mem", "band"),
            P(None, "band", "mem"),
            P("band", None),
        ),
        out_specs=P(("dom", "mem"), "grid", None),
        check_vma=False,
    )
```

time: 163 us -> 76.6 us (0.47)
  waiting for transfers between devices: 92.3 us -> 13.1 us
  between operations: 13.8 us -> 0.53 us
  blocking collectives: 12.8 us -> 0 us
  matrix products: 13.5 us -> 22.3 us
  starting transfers between devices: 15.7 us -> 22.1 us
  local copies, waits for them, and re-layouts: 6.48 us -> 10.2 us
    psum x2 -> x0, waiting for transfers between devices: 45.2 us -> none  [the longest x1 24.5 us: body(): lax.psum(jnp.dot(hidden, w_back, preferred_element_type=jnp.float32).asty...]
    all_gather x4 -> x0, waiting for transfers between devices: 30.2 us -> none  [the longest x1 16.3 us: body(): w_back = lax.all_gather(mlp_out[0], 'mem', axis=1, tiled=True)]
    ppermute x2 -> x17, starting transfers between devices: 4.28 us -> 22.1 us  [shifted(): return lax.ppermute(block, tuple(axes), pairs)]
    all_to_all x2 -> x0, starting transfers between devices: 11.2 us -> none  [the longest x1 6.34 us: body(): lax.all_to_all(picked.astype(jnp.bfloat16), 'grid', split_axis=0, concat_...]
    dot_general x7 -> x16, matrix products: 13.5 us -> 22.3 us  [the longest x14 17.5 us: matmul(): return jnp.dot(left, right, preferred_element_type=F32)]
    all_to_all x2 -> x0, waiting for transfers between devices: 8.14 us -> none  [the longest x1 5.56 us: body(): lax.all_to_all(outgoing.astype(jnp.bfloat16), 'grid', split_axis=0, conca...]
    psum x1 -> x0, blocking collectives: 7.13 us -> none  [body(): lax.psum(jnp.dot(mesh_cols, decode_weight, preferred_element_type=jnp.flo...]
    ppermute x2 -> x17, waiting for transfers between devices: 6.95 us -> 13.1 us  [shifted(): return lax.ppermute(block, tuple(axes), pairs)]
  transfers between devices with their start and end apart: 10 -> 17, of which waited for: 8 -> 4; matrix products, arithmetic and copies ran while one was open for 7% -> 38% of each run, Pallas kernels for 0% -> 0%
where the time goes in v1:
time: 76.6 us; the launch traced here: 76 us
  matrix products  22.3 us (29%)
  starting transfers between devices  22.1 us (29%)
  waiting for transfers between devices  13.1 us (17%)
  local copies, waits for them, and re-layouts  10.2 us (13%)
  other arithmetic  7.77 us (10%)
    ppermute x17, starting transfers between devices, shifted(): return lax.ppermute(block, tuple(axes), pairs)  22.1 us
    dot_general x14, matrix products, matmul(): return jnp.dot(left, right, preferred_element_type=F32)  17.5 us
    ppermute x17, waiting for transfers between devices, shifted(): return lax.ppermute(block, tuple(axes), pairs)  13.1 us
    unnamed x37, local copies, waits for them, and re-layouts  4.9 us
    add x1, local copies, waits for them, and re-layouts, body(): sum((matmul(normed[:, step * model_half:(step + 1) * model_half], part.re...  3.03 us
    dot_general x1, matrix products, body(): jnp.einsum('qhd,khd->hqk', queries, keys, preferred_element_type=F32)  2.69 us
    reduce_sum x3, other arithmetic, rms_norm(): jnp.mean(values * values, axis=-1, keepdims=True) + 1e-06  2.47 us
    unnamed x2, other arithmetic  2.08 us
  transfers between devices with their start and end apart: 17, of which 4 were waited for; matrix products, arithmetic and copies ran while one was open for 38% of the time, Pallas kernels for 0%

profile of v1, /device:TPU:0, one launch (start us, length us, event | category | flops | bytes accessed | tf_op | source)
XLA Modules:
  0.0 76.0 jit_solution(13261323023161336559)
XLA Ops:
  2.9 1.2 %convolution_convert_fusion.3 = bf16[384,128]{1,0:T(8,128)(2,1)S(1)} fusion(s32[384]{0:T(512)S(1)} %pad_add_fusion.2, bf16[1,512,128]{2,1,0:T(8,128)(2,1)} %param.13), kind=kOutput, calls=%fused_computation.26 | convolution fusion | flops 50577408 | bytes 230912 | tf_op jit(solution)/shard_map/dot_general | solution.py:15
  4.7 1.4 %fusion.89 = (s32[4,32]{1,0:T(4,128)S(1)}, bf16[4,1,32]{2,1,0:T(2,128)(2,1)S(1)}) fusion(s32[4,1,32]{2,1,0:T(1,128)} %param.17, s32[]{:T(128)} %broadcast.296), kind=kLoop, calls=%fused_computation.177 | loop fusion | flops 128 | bytes 1284 | tf_op args[4]
  6.2 5.1 %collective-permute-start.1 = (bf16[112,128]{1,0:T(8,128)(2,1)S(1)}, bf16[112,128]{1,0:T(8,128)(2,1)S(1)}, u32[]{:S(2)}, u32[]{:S(2)}) collective-permute-start(bf16[112,128]{1,0:T(8,128)(2,1)S(1)} %get-tuple-element.19), channel_id=1, source_target_pairs={{0,12},{4,0},{8,4},{12,8},{1,13},{5,1},{9,5},{13,9},{2,14},{6,2},{... | collective-permute-start | bytes 86024 | tf_op jit(solution)/shard_map/ppermute | solution.py:34
  12.5 1.5 %collective-permute-start.3 = (bf16[128,512]{1,0:T(8,128)(2,1)}, bf16[128,512]{1,0:T(8,128)(2,1)S(1)}, u32[]{:S(2)}, u32[]{:S(2)}) collective-permute-start(bf16[128,512]{1,0:T(8,128)(2,1)} %param.20), channel_id=1, source_target_pairs={{0,2},{2,0},{1,3},{3,1},{4,6},{6,4},{5,7},{7,5},{8,10},{10,8},{9,1... | collective-permute-start | bytes 393224 | tf_op jit(solution)/shard_map/ppermute | solution.py:34
  14.0 2.6 %copy.23 = bf16[1,512,3,512]{1,3,2,0:T(8,128)(2,1)} copy(bf16[1,512,3,512]{3,1,2,0:T(8,128)(2,1)} %param.21) | data formatting | bytes 3145728 | tf_op args[8]
  22.2 3.7 %collective-permute-done.8 = bf16[512,128]{1,0:T(8,128)(2,1)S(1)} collective-permute-done((bf16[512,128]{1,0:T(8,128)(2,1)S(1)}, bf16[512,128]{1,0:T(8,128)(2,1)S(1)}, u32[]{:S(2)}, u32[]{:S(2)}) %collective-permute-start.8) | collective-permute-done | bytes 131104 | tf_op jit(solution)/shard_map/ppermute | solution.py:34
  27.3 3.2 %convolution_add_fusion = f32[256,1536]{1,0:T(8,128)} fusion(f32[256,1536]{1,0:T(8,128)S(1)} %fusion.36, bf16[512,1536]{0,1:T(8,128)(2,1)} %bitcast.9, bf16[256,1024]{1,0:T(8,128)(2,1)S(1)} %multiply_convert_fusion), kind=kOutput, calls=%fused_computation | convolution fusion | flops 403046400 | bytes 4980736 | tf_op jit(solution)/shard_map/dot_general | solution.py:15
  30.5 3.0 %copy.25 = f32[256,1536]{0,1:T(8,128)} copy(f32[256,1536]{1,0:T(8,128)} %convolution_add_fusion) | data formatting | bytes 3145728 | tf_op jit(solution)/shard_map/add | solution.py:168
  33.5 1.1 %multiply_reduce_fusion.2 = f32[256,8]{0,1:T(8,128)S(1)} fusion(f32[256,3,8,64]{0,3,2,1:T(8,128)} %bitcast.73), kind=kLoop, calls=%fused_computation.53 | loop fusion | flops 260096 | bytes 532480 | tf_op jit(solution)/shard_map/reduce_sum | solution.py:50
  34.6 1.2 %multiply_reduce_fusion.3 = f32[128,8]{0,1:T(8,128)S(1)} fusion(f32[256,3,8,64]{0,3,2,1:T(8,128)} %bitcast.74), kind=kLoop, calls=%fused_computation.78 | loop fusion | flops 130048 | bytes 266240 | tf_op jit(solution)/shard_map/reduce_sum | solution.py:50
  35.8 2.7 %fusion.10 = f32[8,128,256]{2,1,0:T(8,128)} fusion(pred[128,256]{1,0:T(8,128)(4,1)S(1)} %fusion.61, f32[256,3,8,64]{0,3,2,1:T(8,128)} %bitcast.75, f32[256,8]{0,1:T(8,128)S(1)} %add_rsqrt_fusion, f32[128,8]{0,1:T(8,128)S(1)} %add_rsqrt_fusion.1), kind=kOutput, calls=%fused_computation.17 | convolution fusion | flops 34471936 | bytes 1880064 | tf_op jit(solution)/shard_map/qhd,khd->hqk/dot_general | solution.py:185
  38.5 2.1 %convolution_convert_fusion.2 = bf16[8,64,128]{2,1,0:T(8,128)(2,1)S(1)} fusion(f32[8,128,256]{2,1,0:T(8,128)} %fusion.10, f32[256,3,8,64]{0,3,2,1:T(8,128)} %bitcast.76), kind=kOutput, calls=%fused_computation.25 | convolution fusion | flops 34145536 | bytes 2490368 | tf_op jit(solution)/shard_map/hqk,khd->qhd/dot_general | solution.py:190
  40.6 1.3 %convolution_convert_fusion.1 = bf16[128,512]{1,0:T(8,128)(2,1)S(1)} fusion(bf16[128,512]{0,1:T(8,128)(2,1)S(1)} %bitcast.80, bf16[1,512,512]{2,1,0:T(8,128)(2,1)} %param.22), kind=kOutput, calls=%fused_computation.24 | convolution fusion | flops 67174400 | bytes 786432 | tf_op jit(solution)/shard_map/dot_general | solution.py:15
  41.9 1.3 %convolution_convert_fusion = bf16[128,512]{1,0:T(8,128)(2,1)S(1)} fusion(bf16[128,512]{0,1:T(8,128)(2,1)S(1)} %bitcast.81, bf16[512,512]{1,0:T(8,128)(2,1)} %collective-permute-done.5), kind=kOutput, calls=%fused_computation.23 | convolution fusion | flops 67174400 | bytes 786432 | tf_op jit(solution)/shard_map/dot_general | solution.py:15
  44.8 6.4 %collective-permute-done.6 = bf16[128,1024]{1,0:T(8,128)(2,1)S(1)} collective-permute-done((bf16[128,1024]{1,0:T(8,128)(2,1)S(1)}, bf16[128,1024]{1,0:T(8,128)(2,1)S(1)}, u32[]{:S(2)}, u32[]{:S(2)}) %collective-permute-start.6) | collective-permute-done | bytes 262176 | tf_op jit(solution)/shard_map/ppermute | solution.py:34
  51.7 1.2 %copy-done.4 = bf16[1,512,2048]{2,1,0:T(8,128)(2,1)S(1)} copy-done((bf16[1,512,2048]{2,1,0:T(8,128)(2,1)S(1)}, bf16[1,512,2048]{2,1,0:T(8,128)(2,1)}, u32[]{:S(2)}) %copy-start.4) | copy-done | bytes 2097176
  53.4 3.2 %fusion.25 = bf16[128,2048]{1,0:T(8,128)(2,1)} fusion(f32[128,2048]{1,0:T(8,128)S(1)} %fusion.56, bf16[512,2048]{1,0:T(8,128)(2,1)} %collective-permute-done.7, bf16[128,1024]{1,0:T(8,128)(2,1)S(1)} %multiply_convert_fusion.1), kind=kOutput, calls=%fused_computation.39 | convolution fusion | flops 271056896 | bytes 3801088 | tf_op jit(solution)/shard_map/dot_general | solution.py:15
  56.6 1.8 %fusion.17 = bf16[128,128]{1,0:T(8,128)(2,1)S(1)} fusion(f32[128,128]{1,0:T(8,128)S(1)} %fusion.32, bf16[128,2048]{1,0:T(8,128)(2,1)} %fusion.25, f32[2048,128]{0,1:T(8,128)S(1)} %copy-done.3, f32[2048,128]{0,1:T(8,128)} %collective-permute-done.9, f32[128]{0:T(128)S(1)} %broadcast_select_fusion.6, s32[128]{0:T(128)S(1)} %eq.103), kind=kOutput, calls=%fused_computation.31 | convolution fusion | flops 71909376 | bytes 2720768 | tf_op jit(solution)/shard_map/dot_general | solution.py:15
  58.4 3.4 %collective-permute-start.10 = (bf16[32,128]{1,0:T(8,128)(2,1)S(1)}, bf16[32,128]{1,0:T(8,128)(2,1)S(1)}, u32[]{:S(2)}, u32[]{:S(2)}) collective-permute-start(bf16[32,128]{1,0:T(8,128)(2,1)S(1)} %get-tuple-element.17), channel_id=1, source_target_pairs={{0,4},{2,6},{4,8},{6,10},{8,12},{10,14},{12,0},{14,2},{1,5},{3,7},... | collective-permute-start | bytes 24584 | tf_op jit(solution)/shard_map/ppermute | solution.py:34
  62.9 2.9 %collective-permute-start.15 = (bf16[32,128]{1,0:T(8,128)(2,1)S(1)}, bf16[32,128]{1,0:T(8,128)(2,1)S(1)}, u32[]{:S(2)}, u32[]{:S(2)}) collective-permute-start(bf16[32,128]{1,0:T(8,128)(2,1)S(1)} %get-tuple-element.16), channel_id=1, source_target_pairs={{0,10},{2,8},{4,14},{6,12},{8,2},{10,0},{12,6},{14,4},{1,11},{3,9}... | collective-permute-start | bytes 24584 | tf_op jit(solution)/shard_map/ppermute | solution.py:34
  65.8 3.8 %collective-permute-start.12 = (bf16[32,128]{1,0:T(8,128)(2,1)S(1)}, bf16[32,128]{1,0:T(8,128)(2,1)S(1)}, u32[]{:S(2)}, u32[]{:S(2)}) collective-permute-start(bf16[32,128]{1,0:T(8,128)(2,1)S(1)} %get-tuple-element.15), channel_id=1, source_target_pairs={{0,12},{2,14},{4,0},{6,2},{8,4},{10,6},{12,8},{14,10},{1,13},{3,15... | collective-permute-start | bytes 24584 | tf_op jit(solution)/shard_map/ppermute | solution.py:34
  69.6 1.5 %collective-permute-start.13 = (bf16[32,128]{1,0:T(8,128)(2,1)S(1)}, bf16[32,128]{1,0:T(8,128)(2,1)S(1)}, u32[]{:S(2)}, u32[]{:S(2)}) collective-permute-start(bf16[32,128]{1,0:T(8,128)(2,1)S(1)} %get-tuple-element.6), channel_id=1, source_target_pairs={{0,2},{2,0},{4,6},{6,4},{8,10},{10,8},{12,14},{14,12},{1,3},{3,1},... | collective-permute-start | bytes 24584 | tf_op jit(solution)/shard_map/ppermute | solution.py:34
  71.1 2.2 %collective-permute-done.13 = bf16[32,128]{1,0:T(8,128)(2,1)S(1)} collective-permute-done((bf16[32,128]{1,0:T(8,128)(2,1)S(1)}, bf16[32,128]{1,0:T(8,128)(2,1)S(1)}, u32[]{:S(2)}, u32[]{:S(2)}) %collective-permute-start.13) | collective-permute-done | bytes 8224 | tf_op jit(solution)/shard_map/ppermute | solution.py:34
  74.1 1.9 %fusion.15 = bf16[1,512,128]{2,1,0:T(8,128)(2,1)} fusion(bf16[256,128]{1,0:T(8,128)(2,1)S(1)} %constant_dynamic-update-slice_fusion, pred[512,128]{1,0:T(32,128)(4,1)S(1)} %iota_compare_fusion.3, bf16[512,128]{1,0:T(8,128)(2,1)} %param.14, bf16[1,512,128]{2,1,0:T(8,128)(2,1)} %param.13, pred[512]{0:T(512)(128)(4,1)S(1)} %broadcast_compare_fusion), kind=kOutput, calls=%fused_computation.27 | convolution fusion | flops 34013184 | bytes 524800 | tf_op jit(solution)/shard_map/dot_general | solution.py:15
  (132 shorter events, 15.9 us)
Async XLA Ops:
  0.0 43.8 %copy-start = (bf16[1,2048,512]{2,1,0:T(8,128)(2,1)S(1)}, bf16[1,2048,512]{2,1,0:T(8,128)(2,1)}, u32[]{:S(2)}) copy-start(bf16[1,2048,512]{2,1,0:T(8,128)(2,1)} %param.24) | copy-start | bytes 6291460
  6.2 12.4 %collective-permute-start.1 = (bf16[112,128]{1,0:T(8,128)(2,1)S(1)}, bf16[112,128]{1,0:T(8,128)(2,1)S(1)}, u32[]{:S(2)}, u32[]{:S(2)}) collective-permute-start(bf16[112,128]{1,0:T(8,128)(2,1)S(1)} %get-tuple-element.19), channel_id=1, source_target_pairs={{0,12},{4,0},{8,4},{12,8},{1,13},{5,1},{9,5},{13,9},{2,14},{6,2},{... | collective-permute-start | bytes 86024 | tf_op jit(solution)/shard_map/ppermute | solution.py:34
  11.4 7.9 %collective-permute-start = (bf16[112,128]{1,0:T(8,128)(2,1)S(1)}, bf16[112,128]{1,0:T(8,128)(2,1)S(1)}, u32[]{:S(2)}, u32[]{:S(2)}) collective-permute-start(bf16[112,128]{1,0:T(8,128)(2,1)S(1)} %get-tuple-element.18), channel_id=1, source_target_pairs={{0,4},{4,8},{8,12},{12,0},{1,5},{5,9},{9,13},{13,1},{2,6},{6,10},{... | collective-permute-start | bytes 86024 | tf_op jit(solution)/shard_map/ppermute | solution.py:34
  11.4 6.9 %copy-start.12 = (s32[512]{0:T(512)S(1)}, s32[512]{0:T(512)}, u32[]{:S(2)}) copy-start(s32[512]{0:T(512)} %param.15) | copy-start | bytes 6148
  11.4 8.0 %copy-start.10 = (s32[4,1,32]{2,1,0:T(1,128)S(1)}, s32[4,1,32]{2,1,0:T(1,128)}, u32[]{:S(2)}) copy-start(s32[4,1,32]{2,1,0:T(1,128)} %param.17) | copy-start | bytes 1540
  11.4 8.5 %copy-start.6 = (bf16[512,128]{1,0:T(8,128)(2,1)S(1)}, bf16[512,128]{1,0:T(8,128)(2,1)}, u32[]{:S(2)}) copy-start(bf16[512,128]{1,0:T(8,128)(2,1)} %param.25) | copy-start | bytes 393220
  11.4 9.1 %copy-start.5 = (bf16[128,512]{1,0:T(8,128)(2,1)S(1)}, bf16[128,512]{1,0:T(8,128)(2,1)}, u32[]{:S(2)}) copy-start(bf16[128,512]{1,0:T(8,128)(2,1)} %param.20) | copy-start | bytes 393220
  11.4 9.1 %collective-permute-start.2 = (bf16[96,128]{1,0:T(8,128)(2,1)S(1)}, bf16[96,128]{1,0:T(8,128)(2,1)S(1)}, u32[]{:S(2)}, u32[]{:S(2)}) collective-permute-start(bf16[96,128]{1,0:T(8,128)(2,1)S(1)} %get-tuple-element.12), channel_id=1, source_target_pairs={{0,8},{4,12},{8,0},{12,4},{1,9},{5,13},{9,1},{13,5},{2,10},{6,14},... | collective-permute-start | bytes 73736 | tf_op jit(solution)/shard_map/ppermute | solution.py:34
  12.5 7.4 %collective-permute-start.3 = (bf16[128,512]{1,0:T(8,128)(2,1)}, bf16[128,512]{1,0:T(8,128)(2,1)S(1)}, u32[]{:S(2)}, u32[]{:S(2)}) collective-permute-start(bf16[128,512]{1,0:T(8,128)(2,1)} %param.20), channel_id=1, source_target_pairs={{0,2},{2,0},{1,3},{3,1},{4,6},{6,4},{5,7},{7,5},{8,10},{10,8},{9,1... | collective-permute-start | bytes 393224 | tf_op jit(solution)/shard_map/ppermute | solution.py:34
  16.6 10.8 %collective-permute-start.4 = (bf16[512,3,512]{0,2,1:T(8,128)(2,1)}, bf16[512,3,512]{0,2,1:T(8,128)(2,1)}, u32[]{:S(2)}, u32[]{:S(2)}) collective-permute-start(bf16[512,3,512]{0,2,1:T(8,128)(2,1)} %bitcast.77), channel_id=1, source_target_pairs={{0,1},{1,0},{2,3},{3,2},{4,5},{5,4},{6,7},{7,6},{8,9},{9,8},{10,11... | collective-permute-start | bytes 4718600 | tf_op jit(solution)/shard_map/ppermute | solution.py:34
  18.6 23.3 %collective-permute-start.5 = (bf16[512,512]{1,0:T(8,128)(2,1)}, bf16[512,512]{1,0:T(8,128)(2,1)}, u32[]{:S(2)}, u32[]{:S(2)}) collective-permute-start(bf16[512,512]{1,0:T(8,128)(2,1)} %bitcast.16), channel_id=1, source_target_pairs={{0,1},{1,0},{2,3},{3,2},{4,5},{5,4},{6,7},{7,6},{8,9},{9,8},{10,11... | collective-permute-start | bytes 1572872 | tf_op jit(solution)/shard_map/ppermute | solution.py:34
  19.2 34.2 %collective-permute-start.7 = (bf16[512,2048]{1,0:T(8,128)(2,1)}, bf16[512,2048]{1,0:T(8,128)(2,1)}, u32[]{:S(2)}, u32[]{:S(2)}) collective-permute-start(bf16[512,2048]{1,0:T(8,128)(2,1)} %bitcast.79), channel_id=1, source_target_pairs={{0,1},{1,0},{2,3},{3,2},{4,5},{5,4},{6,7},{7,6},{8,9},{9,8},{10,11... | collective-permute-start | bytes 6291464 | tf_op jit(solution)/shard_map/ppermute | solution.py:34
  19.9 6.0 %collective-permute-start.8 = (bf16[512,128]{1,0:T(8,128)(2,1)S(1)}, bf16[512,128]{1,0:T(8,128)(2,1)S(1)}, u32[]{:S(2)}, u32[]{:S(2)}) collective-permute-start(bf16[512,128]{1,0:T(8,128)(2,1)S(1)} %copy-done.6), channel_id=1, source_target_pairs={{0,2},{2,0},{1,3},{3,1},{4,6},{6,4},{5,7},{7,5},{8,10},{10,8},{9,1... | collective-permute-start | bytes 393224 | tf_op jit(solution)/shard_map/ppermute | solution.py:34
  43.2 7.9 %collective-permute-start.6 = (bf16[128,1024]{1,0:T(8,128)(2,1)S(1)}, bf16[128,1024]{1,0:T(8,128)(2,1)S(1)}, u32[]{:S(2)}, u32[]{:S(2)}) collective-permute-start(bf16[128,1024]{1,0:T(8,128)(2,1)S(1)} %pad_maximum_fusion), channel_id=1, source_target_pairs={{0,2},{2,0},{1,3},{3,1},{4,6},{6,4},{5,7},{7,5},{8,10},{10,8},{9,1... | collective-permute-start | bytes 786440 | tf_op jit(solution)/shard_map/ppermute | solution.py:34
  43.8 7.5 %copy-start.7 = (bf16[512,128]{1,0:T(8,128)(2,1)S(1)}, bf16[512,128]{1,0:T(8,128)(2,1)}, u32[]{:S(2)}) copy-start(bf16[512,128]{1,0:T(8,128)(2,1)} %get-tuple-element.10) | copy-start | bytes 393220
  44.7 7.1 %copy-start.2 = (f32[2048,128]{0,1:T(8,128)}, f32[2048,128]{0,1:T(8,128)S(1)}, u32[]{:S(2)}) copy-start(f32[2048,128]{0,1:T(8,128)S(1)} %convolution_bitcast_fusion) | copy-start | bytes 3145732
  44.7 11.9 %collective-permute-start.9 = (f32[2048,128]{0,1:T(8,128)S(1)}, f32[2048,128]{0,1:T(8,128)}, u32[]{:S(2)}, u32[]{:S(2)}) collective-permute-start(f32[2048,128]{0,1:T(8,128)S(1)} %convolution_bitcast_fusion), channel_id=1, source_target_pairs={{0,1},{1,0},{2,3},{3,2},{4,5},{5,4},{6,7},{7,6},{8,9},{9,8},{10,11... | collective-permute-start | bytes 3145736 | tf_op jit(solution)/shard_map/ppermute | solution.py:34
  58.4 11.1 %collective-permute-start.10 = (bf16[32,128]{1,0:T(8,128)(2,1)S(1)}, bf16[32,128]{1,0:T(8,128)(2,1)S(1)}, u32[]{:S(2)}, u32[]{:S(2)}) collective-permute-start(bf16[32,128]{1,0:T(8,128)(2,1)S(1)} %get-tuple-element.17), channel_id=1, source_target_pairs={{0,4},{2,6},{4,8},{6,10},{8,12},{10,14},{12,0},{14,2},{1,5},{3,7},... | collective-permute-start | bytes 24584 | tf_op jit(solution)/shard_map/ppermute | solution.py:34
  61.9 11.4 %collective-permute-start.14 = (bf16[32,128]{1,0:T(8,128)(2,1)S(1)}, bf16[32,128]{1,0:T(8,128)(2,1)S(1)}, u32[]{:S(2)}, u32[]{:S(2)}) collective-permute-start(bf16[32,128]{1,0:T(8,128)(2,1)S(1)} %get-tuple-element.17), channel_id=1, source_target_pairs={{0,6},{2,4},{4,10},{6,8},{8,14},{10,12},{12,2},{14,0},{1,7},{3,5},... | collective-permute-start | bytes 24584 | tf_op jit(solution)/shard_map/ppermute | solution.py:34
  61.9 7.7 %collective-permute-start.11 = (bf16[32,128]{1,0:T(8,128)(2,1)S(1)}, bf16[32,128]{1,0:T(8,128)(2,1)S(1)}, u32[]{:S(2)}, u32[]{:S(2)}) collective-permute-start(bf16[32,128]{1,0:T(8,128)(2,1)S(1)} %get-tuple-element.16), channel_id=1, source_target_pairs={{0,8},{2,10},{4,12},{6,14},{8,0},{10,2},{12,4},{14,6},{1,9},{3,11}... | collective-permute-start | bytes 24584 | tf_op jit(solution)/shard_map/ppermute | solution.py:34
  62.9 10.4 %collective-permute-start.15 = (bf16[32,128]{1,0:T(8,128)(2,1)S(1)}, bf16[32,128]{1,0:T(8,128)(2,1)S(1)}, u32[]{:S(2)}, u32[]{:S(2)}) collective-permute-start(bf16[32,128]{1,0:T(8,128)(2,1)S(1)} %get-tuple-element.16), channel_id=1, source_target_pairs={{0,10},{2,8},{4,14},{6,12},{8,2},{10,0},{12,6},{14,4},{1,11},{3,9}... | collective-permute-start | bytes 24584 | tf_op jit(solution)/shard_map/ppermute | solution.py:34
  65.8 5.3 %collective-permute-start.12 = (bf16[32,128]{1,0:T(8,128)(2,1)S(1)}, bf16[32,128]{1,0:T(8,128)(2,1)S(1)}, u32[]{:S(2)}, u32[]{:S(2)}) collective-permute-start(bf16[32,128]{1,0:T(8,128)(2,1)S(1)} %get-tuple-element.15), channel_id=1, source_target_pairs={{0,12},{2,14},{4,0},{6,2},{8,4},{10,6},{12,8},{14,10},{1,13},{3,15... | collective-permute-start | bytes 24584 | tf_op jit(solution)/shard_map/ppermute | solution.py:34
  69.5 4.6 %collective-permute-start.16 = (bf16[32,128]{1,0:T(8,128)(2,1)S(1)}, bf16[32,128]{1,0:T(8,128)(2,1)S(1)}, u32[]{:S(2)}, u32[]{:S(2)}) collective-permute-start(bf16[32,128]{1,0:T(8,128)(2,1)S(1)} %get-tuple-element.15), channel_id=1, source_target_pairs={{0,14},{2,12},{4,2},{6,0},{8,6},{10,4},{12,10},{14,8},{1,15},{3,13... | collective-permute-start | bytes 24584 | tf_op jit(solution)/shard_map/ppermute | solution.py:34
  69.6 3.7 %collective-permute-start.13 = (bf16[32,128]{1,0:T(8,128)(2,1)S(1)}, bf16[32,128]{1,0:T(8,128)(2,1)S(1)}, u32[]{:S(2)}, u32[]{:S(2)}) collective-permute-start(bf16[32,128]{1,0:T(8,128)(2,1)S(1)} %get-tuple-element.6), channel_id=1, source_target_pairs={{0,2},{2,0},{4,6},{6,4},{8,10},{10,8},{12,14},{14,12},{1,3},{3,1},... | collective-permute-start | bytes 24584 | tf_op jit(solution)/shard_map/ppermute | solution.py:34
  (6 other events, 25.2 us)

commit v2 on v0

v2 whole, which is shorter than its diff:
```python
import functools

import jax
import jax.numpy as jnp
from jax import lax
from jax.experimental import pallas as pl
from jax.experimental.pallas import tpu as pltpu
from jax.sharding import PartitionSpec as P

HEADS = 16
M_DEV = 128
WINDOW = 64
EXTENT = M_DEV + 2 * WINDOW
DIRECT_PEERS = 8
CHUNKS = 4
LANES = 128
BF16 = jnp.bfloat16
F32 = jnp.float32
VMEM = pl.BlockSpec(memory_space=pltpu.VMEM)
ANY = pl.BlockSpec(memory_space=pl.ANY)


def matmul(left, right):
    return jnp.dot(left, right, preferred_element_type=F32)


def matmul_rows(left, right):
    return lax.dot_general(left, right, (((0,), (0,)), ((), ())), preferred_element_type=F32)


def matmul_cols(left, right):
    return lax.dot_general(left, right, (((1,), (1,)), ((), ())), preferred_element_type=F32)


def shifted(block, axis, step):
    count = lax.axis_size(axis)
    return lax.ppermute(block, axis, [(at, (at + step) % count) for at in range(count)])


def ring(block, axis):
    return [block] + [shifted(block, axis, step) for step in range(1, lax.axis_size(axis))]


def choose(options, index):
    picked = options[0]
    for at in range(1, len(options)):
        picked = jnp.where(index == at, options[at], picked)
    return picked


def mem_order(got, mems):
    bands = len(got)
    band_at, mem_at = lax.axis_index("band"), lax.axis_index("mem")
    pieces = bands // mems
    parts = []
    for step in range(mems):
        for inner in range(pieces):
            shard = lax.rem(mem_at - step + mems, mems) * pieces + inner
            parts.append(choose(got, lax.rem(band_at - shard + bands, bands)))
    return parts


def rms_norm(values):
    return values * lax.rsqrt(jnp.mean(values * values, axis=-1, keepdims=True) + 1e-06)


def hi_lo(values):
    high = values.astype(BF16)
    return high, (values - high.astype(F32)).astype(BF16)


def iota(shape, dim):
    return lax.broadcasted_iota(jnp.int32, shape, dim)


def column(values):
    count, slots = values.shape
    tall = jnp.concatenate(
        [jnp.broadcast_to(values[at : at + 1], (slots, slots)) for at in range(count)]
    )
    own = lax.rem(iota(tall.shape, 0), slots) == iota(tall.shape, 1)
    return jnp.sum(jnp.where(own, tall, 0.0), axis=1, keepdims=True)


def live_weights(count_ref, weight_ref):
    weights = weight_ref[...]
    return jnp.where(iota(weights.shape, 1) < count_ref[...], weights, 0.0)


def pick_kernel(src_ref, rows_ref, dst_ref, count_ref, weight_ref, *rest):
    outs, padded, note = rest[:-2], rest[-2], rest[-1]
    shards, slots = src_ref.shape
    span = shards * slots
    grid_at = lax.axis_index("grid")
    home = column(src_ref[...].astype(F32))
    spread = (home == iota((span, rows_ref.shape[0]), 1).astype(F32)).astype(BF16)
    edge = jnp.zeros((slots, rows_ref.shape[1]), BF16)
    padded[0:slots] = edge
    padded[slots : slots + span] = matmul(spread, rows_ref[...]).astype(BF16)
    padded[slots + span :] = edge
    weights = live_weights(count_ref, weight_ref)
    high = weights.astype(BF16).astype(F32)
    note[...] = jnp.zeros(note.shape, F32)
    note[0:shards, 0:slots] = dst_ref[...].astype(F32)
    note[shards : 2 * shards, 0:slots] = high
    note[2 * shards : 3 * shards, 0:slots] = weights - high
    packed = note[...].astype(BF16)
    for at, out in enumerate(outs):
        towards = lax.rem(grid_at + at, shards) if len(outs) <= DIRECT_PEERS else at
        out[0 : 3 * slots] = padded[pl.ds(pl.multiple_of(towards * slots, slots), 3 * slots)]
        out[3 * slots :] = packed


def attend_kernel(shards, bands, mems, direct, *refs):
    refs = list(refs)
    messages = [refs.pop(0) for _ in range(shards)]
    below, above, dst_ref, count_ref, weight_ref = (refs.pop(0) for _ in range(5))
    embeds = [refs.pop(0) for _ in range(bands)]
    qkv_hbm = [refs.pop(0) for _ in range(mems)]
    out_hbm = [refs.pop(0) for _ in range(mems)]
    product_ref, resid_ref, arrived, qkv, proj, sems = refs
    slots = dst_ref.shape[1]
    grid_at = lax.axis_index("grid")
    copies = [pltpu.make_async_copy(s, qkv.at[i], sems.at[i]) for i, s in enumerate(qkv_hbm)]
    copies += [
        pltpu.make_async_copy(s, proj.at[i], sems.at[mems + i]) for i, s in enumerate(out_hbm)
    ]
    for copy in copies:
        copy.start()

    for step, message in enumerate(messages):
        origin = lax.rem(grid_at - step + shards, shards) if direct else step
        arrived[pl.ds(pl.multiple_of(origin * 3 * slots, 3 * slots), 3 * slots)] = message[
            0 : 3 * slots
        ]
    places, loads = [], []
    for offset, message in ((-M_DEV, below), (0, None), (M_DEV, above)):
        if message is None:
            places.append(dst_ref[...].astype(F32) + WINDOW)
            loads.append(live_weights(count_ref, weight_ref))
        else:
            inside = grid_at > 0 if offset < 0 else grid_at < shards - 1
            note = message[3 * slots :].astype(F32)
            places.append(note[0:shards, 0:slots] + (WINDOW + offset))
            load = note[shards : 2 * shards, 0:slots] + note[2 * shards : 3 * shards, 0:slots]
            loads.append(jnp.where(inside, load, 0.0))
    order = [(c, s) for s in range(shards) for c in range(3)]
    place = column(jnp.concatenate([places[c][s : s + 1] for c, s in order]))
    load = column(jnp.concatenate([loads[c][s : s + 1] for c, s in order]))
    spread = jnp.where(place == iota((place.shape[0], EXTENT), 1).astype(F32), load, 0.0)
    spread_high, spread_low = hi_lo(spread)
    embed = jnp.concatenate(mem_order([ref[...] for ref in embeds], mems), axis=1)
    embedded = jax.nn.gelu(matmul(arrived[...], embed)).astype(BF16)
    mesh_in = matmul_rows(spread_high, embedded) + matmul_rows(spread_low, embedded)
    mesh_in = mesh_in.astype(BF16)
    resid_ref[...] = mesh_in[WINDOW : WINDOW + M_DEV]
    normed = rms_norm(mesh_in.astype(F32)).astype(BF16)

    half = qkv.shape[2]
    width = qkv.shape[3]
    head_dim = half * mems // HEADS
    for copy in copies[:mems]:
        copy.wait()

    def project(rows, which):
        return sum(
            matmul(rows[:, step * half : (step + 1) * half], qkv[step, which])
            for step in range(mems)
        )

    queries = project(normed[WINDOW : WINDOW + M_DEV], 0)
    keys = project(normed, 1)
    values = project(normed, 2).astype(BF16)
    group = LANES // head_dim
    same = (iota((LANES, LANES), 0) // head_dim == iota((LANES, LANES), 1) // head_dim).astype(BF16)
    lane_head = iota((M_DEV, LANES), 1) // head_dim

    def head_norm(block):
        mean = matmul((block * block).astype(BF16), same) * (1.0 / head_dim)
        return (block * lax.rsqrt(mean + 1e-06)).astype(BF16)

    row = iota((M_DEV, EXTENT), 0)
    col = iota((M_DEV, EXTENT), 1)
    key_pos = grid_at * M_DEV - WINDOW + col
    visible = (
        (jnp.abs(row + WINDOW - col) <= WINDOW) & (key_pos >= 0) & (key_pos < M_DEV * shards)
    )
    visible = jnp.concatenate([visible.astype(F32)] * group)
    attended = []
    for block in range(width // LANES):
        lanes = slice(block * LANES, (block + 1) * LANES)
        query = head_norm(queries[:, lanes])
        key = head_norm(keys[:, lanes])
        stacked = jnp.concatenate(
            [jnp.where(lane_head == head, query, jnp.zeros_like(query)) for head in range(group)]
        )
        scores = matmul_cols(stacked, key) * head_dim ** (-0.5)
        weights = jnp.exp(scores) * visible
        shares = (weights / jnp.sum(weights, axis=-1, keepdims=True)).astype(BF16)
        mixed = matmul(shares, values[:, lanes])
        attended.append(
            choose([mixed[head * M_DEV : (head + 1) * M_DEV] for head in range(group)], lane_head)
        )
    attended = jnp.concatenate(attended, axis=1).astype(BF16)
    for copy in copies[mems:]:
        copy.wait()
    for step in range(mems):
        product_ref[:, step * half : (step + 1) * half] = matmul(attended, proj[step]).astype(BF16)


def fold_kernel(back_ref, *refs):
    decodes, out_ref = refs[:-1], refs[-1]
    mems = lax.axis_size("mem")
    decode = jnp.concatenate(mem_order([ref[...] for ref in decodes], mems)[: len(decodes) // mems])
    out_ref[...] = matmul(back_ref[...], decode)


def finish_kernel(shards, bands, mems, copies_out, *refs):
    refs = list(refs)
    products = [refs.pop(0) for _ in range(bands)]
    resid_ref = refs.pop(0)
    in_hbm = [refs.pop(0) for _ in range(mems)]
    folds = [refs.pop(0) for _ in range(mems)]
    decodes = [refs.pop(0) for _ in range(bands)]
    dst_ref, count_ref, weight_ref, out_ref, weight_in, sems = refs
    half, hidden_width = weight_in.shape[1:]
    step_width = hidden_width // CHUNKS
    slots = dst_ref.shape[1]

    def fetch(chunk, at):
        lanes = pl.ds(chunk * step_width, step_width)
        return pltpu.make_async_copy(
            in_hbm[at].at[:, lanes], weight_in.at[at, :, lanes], sems.at[chunk, at]
        )

    for chunk in range(CHUNKS):
        for at in range(mems):
            fetch(chunk, at).start()
    stream = resid_ref[...].astype(F32) + sum(ref[...].astype(F32) for ref in products)
    normed = rms_norm(stream).astype(BF16)
    reach = (column(dst_ref[...].astype(F32)) == iota((shards * slots, M_DEV), 1).astype(F32)).astype(
        BF16
    )
    load = column(live_weights(count_ref, weight_ref))
    carried = jnp.where(lax.axis_index("band") == 0, stream, 0.0).astype(BF16)
    decode = jnp.concatenate(mem_order([ref[...] for ref in decodes], mems))
    projected = matmul(carried, decode)
    for chunk in range(CHUNKS):
        lanes = slice(chunk * step_width, (chunk + 1) * step_width)
        for at in range(mems):
            fetch(chunk, at).wait()
        hidden = jax.nn.gelu(
            sum(
                matmul(normed[:, at * half : (at + 1) * half], weight_in[at, :, lanes])
                for at in range(mems)
            )
        ).astype(BF16)
        fold = sum(ref[lanes, :] for ref in folds).astype(BF16)
        projected = projected + matmul(hidden, fold)
    outgoing = (matmul(reach, projected.astype(BF16)) * load).astype(BF16)
    for shard in range(shards):
        for at in range(copies_out):
            out_ref[shard * copies_out + at] = outgoing[shard * slots : (shard + 1) * slots]


def body(
    grid_state,
    forcing,
    boundary_mask,
    edge_src,
    edge_dst,
    edge_count,
    edge_weight,
    embed_weight,
    attn_qkv,
    attn_out,
    mlp_in,
    mlp_out,
    decode_weight,
):
    shards, bands, mems = (lax.axis_size(axis) for axis in ("grid", "band", "mem"))
    direct = shards <= DIRECT_PEERS
    grid_at = lax.axis_index("grid")
    rows = grid_state[0]
    points, channels = rows.shape
    sources, targets, weights = edge_src[0], edge_dst[:, 0], edge_weight[:, 0]
    slots = targets.shape[1]
    qkv_own = jnp.transpose(attn_qkv[0], (1, 0, 2))
    half, width = qkv_own.shape[1:]
    model = half * mems
    edges = (targets, edge_count, weights)
    note_rows = -(-3 * shards // 16) * 16
    message_shape = jax.ShapeDtypeStruct((3 * slots + note_rows, channels), BF16)

    messages = pl.pallas_call(
        pick_kernel,
        out_shape=[message_shape] * shards,
        in_specs=[VMEM] * 5,
        out_specs=[VMEM] * shards,
        scratch_shapes=[
            pltpu.VMEM(((shards + 2) * slots, channels), BF16),
            pltpu.VMEM((note_rows, channels), F32),
        ],
        name="pick",
    )(sources, rows, *edges)
    if direct:
        messages = [messages[0]] + [
            shifted(messages[step], "grid", step) for step in range(1, shards)
        ]
        below, above = messages[1 % shards], messages[shards - 1]
    else:
        stacked = lax.all_to_all(jnp.stack(messages), "grid", 0, 0, tiled=True)
        messages = [stacked[at] for at in range(shards)]
        below = stacked[(grid_at - 1) % shards]
        above = stacked[(grid_at + 1) % shards]

    embeds = ring(embed_weight, "band")
    qkv_parts = ring(qkv_own, "mem")
    out_parts = ring(attn_out[0], "mem")
    in_parts = ring(mlp_in[0], "mem")
    decodes = ring(decode_weight, "band")
    back = mlp_out[0]
    folded = pl.pallas_call(
        fold_kernel,
        out_shape=jax.ShapeDtypeStruct((back.shape[0], channels), F32),
        in_specs=[VMEM] * (1 + bands),
        out_specs=VMEM,
        name="fold",
    )(back, *decodes)
    folds = ring(folded, "mem")

    product, resid = pl.pallas_call(
        functools.partial(attend_kernel, shards, bands, mems, direct),
        out_shape=[jax.ShapeDtypeStruct((M_DEV, model), BF16)] * 2,
        in_specs=[VMEM] * (shards + 5 + bands) + [ANY] * (2 * mems),
        out_specs=[VMEM] * 2,
        scratch_shapes=[
            pltpu.VMEM((shards * 3 * slots, channels), BF16),
            pltpu.VMEM((mems, 3, half, width), BF16),
            pltpu.VMEM((mems, width, half), BF16),
            pltpu.SemaphoreType.DMA((2 * mems,)),
        ],
        name="attend",
    )(*messages, below, above, *edges, *embeds, *qkv_parts, *out_parts)
    products = ring(product, "band")

    hidden_width = mlp_in.shape[2]
    copies_out = bands if direct else 1
    outgoing = pl.pallas_call(
        functools.partial(finish_kernel, shards, bands, mems, copies_out),
        out_shape=jax.ShapeDtypeStruct((shards * copies_out, slots, channels), BF16),
        in_specs=[VMEM] * (bands + 1) + [ANY] * mems + [VMEM] * (mems + bands + 3),
        out_specs=VMEM,
        scratch_shapes=[
            pltpu.VMEM((mems, half, hidden_width), BF16),
            pltpu.SemaphoreType.DMA((CHUNKS, mems)),
        ],
        name="finish",
    )(*products, resid, *in_parts, *folds, *decodes, *edges)
    if direct:
        returned = lax.all_to_all(outgoing, ("grid", "band"), 0, 0, tiled=True)
    else:
        summed = sum(part.astype(F32) for part in ring(outgoing, "band"))
        returned = lax.all_to_all(summed.astype(BF16), "grid", 0, 0, tiled=True)
    returned = returned.reshape(-1, channels)

    home = jnp.broadcast_to(sources[:, None, :], (shards, copies_out, slots)).reshape(-1)
    forced = boundary_mask[:, None] == 1
    place = jnp.arange(points, dtype=jnp.int32)[:, None]
    scatter = ((place == home[None, :]) & ~forced).astype(BF16)
    base = jnp.where(forced, forcing, rows)
    return (base.astype(F32) + matmul(scatter, returned)).astype(BF16)[None]


def solution(mesh):
    return jax.shard_map(
        body,
        mesh=mesh,
        in_specs=(
            P(("dom", "mem"), "grid", None),
            P(("dom", "grid"), None),
            P("grid"),
            P("grid", None, None),
            P(None, "grid", None),
            P(None, "grid"),
            P(None, "grid", None),
            P(None, "band"),
            P(None, "mem", None, "band"),
            P(None, "band", "mem"),
            P(None, "mem", "band"),
            P(None, "band", "mem"),
            P("band", None),
        ),
        out_specs=P(("dom", "mem"), "grid", None),
        check_vma=False,
    )
```

time: 163 us -> 71.2 us (0.44)
  waiting for transfers between devices: 92.3 us -> 28.5 us
  Pallas kernels: 0 us -> 18 us
  between operations: 13.8 us -> 0.08 us
  blocking collectives: 12.8 us -> 0 us
  matrix products: 13.5 us -> 1.84 us
  other arithmetic: 7.68 us -> 0.01 us
  starting transfers between devices: 15.7 us -> 19.1 us
  local copies, waits for them, and re-layouts: 6.48 us -> 3.46 us
    psum x2 -> x0, waiting for transfers between devices: 45.2 us -> none  [the longest x1 24.5 us: body(): lax.psum(jnp.dot(hidden, w_back, preferred_element_type=jnp.float32).asty...]
    all_gather x4 -> x0, waiting for transfers between devices: 30.2 us -> none  [the longest x1 16.3 us: body(): w_back = lax.all_gather(mlp_out[0], 'mem', axis=1, tiled=True)]
    pallas_call x0 -> x4, Pallas kernels: none -> 18 us  [the longest x1 6.74 us: body(): pl.pallas_call(functools.partial(attend_kernel, shards, bands, mems, dire...]
    ppermute x2 -> x10, waiting for transfers between devices: 6.95 us -> 21.6 us  [shifted(): lax.ppermute(block, axis, [(at, (at + step) % count) for at in range(coun...]
    dot_general x7 -> x1, matrix products: 13.5 us -> 1.84 us  [matmul(): return jnp.dot(left, right, preferred_element_type=F32)]
    ppermute x2 -> x10, starting transfers between devices: 4.28 us -> 12.9 us  [shifted(): lax.ppermute(block, axis, [(at, (at + step) % count) for at in range(coun...]
    psum x1 -> x0, blocking collectives: 7.13 us -> none  [body(): lax.psum(jnp.dot(mesh_cols, decode_weight, preferred_element_type=jnp.flo...]
    all_gather x1 -> x0, blocking collectives: 5.64 us -> none  [body(): lax.all_gather(mesh_part.astype(jnp.bfloat16), 'band', axis=1, tiled=True)]
  transfers between devices with their start and end apart: 10 -> 11, of which waited for: 8 -> 7; matrix products, arithmetic and copies ran while one was open for 7% -> 1% of each run, Pallas kernels for 0% -> 17%
where the time goes in v2:
time: 71.2 us; the launch traced here: 70.9 us
  waiting for transfers between devices  28.5 us (40%)
  starting transfers between devices  19.1 us (27%)
  Pallas kernels  18 us (25%)
  local copies, waits for them, and re-layouts  3.46 us (5%)
  matrix products  1.84 us (3%)
    ppermute x10, waiting for transfers between devices, shifted(): lax.ppermute(block, axis, [(at, (at + step) % count) for at in range(coun...  21.6 us
    ppermute x10, starting transfers between devices, shifted(): lax.ppermute(block, axis, [(at, (at + step) % count) for at in range(coun...  12.9 us
    all_to_all x1, waiting for transfers between devices, body(): returned = lax.all_to_all(outgoing, ('grid', 'band'), 0, 0, tiled=True)  6.89 us
    pallas_call x1, Pallas kernels, body(): pl.pallas_call(functools.partial(attend_kernel, shards, bands, mems, dire...  6.74 us
    all_to_all x1, starting transfers between devices, body(): returned = lax.all_to_all(outgoing, ('grid', 'band'), 0, 0, tiled=True)  6.16 us
    pallas_call x1, Pallas kernels, body(): pl.pallas_call(functools.partial(finish_kernel, shards, bands, mems, copi...  6.01 us
    pallas_call x1, Pallas kernels, body(): pl.pallas_call(fold_kernel, out_shape=jax.ShapeDtypeStruct((back.shape[0]...  3.38 us
    unnamed x27, local copies, waits for them, and re-layouts  3.37 us
  transfers between devices with their start and end apart: 11, of which 7 were waited for; matrix products, arithmetic and copies ran while one was open for 1% of the time, Pallas kernels for 17%

profile of v2, /device:TPU:0, one launch (start us, length us, event | category | flops | bytes accessed | tf_op | source)
XLA Modules:
  0.0 70.9 jit_solution(10688717714515407055)
XLA Ops:
  0.6 2.9 %collective-permute-start.8 = (bf16[512,128]{1,0:T(8,128)(2,1)}, bf16[512,128]{1,0:T(8,128)(2,1)S(1)}, u32[]{:S(2)}, u32[]{:S(2)}) collective-permute-start(bf16[512,128]{1,0:T(8,128)(2,1)} %refs_7_.2), channel_id=1, source_target_pairs={{0,2},{2,0},{1,3},{3,1},{4,6},{6,4},{5,7},{7,5},{8,10},{10,8},{9,1... | collective-permute-start | bytes 393224 | tf_op jit(solution)/shard_map/ppermute | solution.py:37
  3.5 3.9 %collective-permute-done.8.refs_1_.refs_8_ = bf16[512,128]{1,0:T(8,128)(2,1)S(1)} collective-permute-done((bf16[512,128]{1,0:T(8,128)(2,1)}, bf16[512,128]{1,0:T(8,128)(2,1)S(1)}, u32[]{:S(2)}, u32[]{:S(2)}) %collective-permute-start.8) | collective-permute-done | bytes 131104 | tf_op jit(solution)/shard_map/ppermute | solution.py:37
  7.4 0.6 copy-done.2
  8.1 3.4 %fold.1.refs_5_ = f32[2048,128]{1,0:T(8,128)} custom-call(bf16[2048,512]{1,0:T(8,128)(2,1)} %bitcast.15, bf16[512,128]{1,0:T(8,128)(2,1)} %refs_7_.2, bf16[512,128]{1,0:T(8,128)(2,1)} %copy-done.2), custom_call_target="tpu_custom_call" | custom-call | tf_op jit(solution)/shard_map/fold/pallas_call | solution.py:323
  12.0 0.7 copy.14.count_ref.refs_7_.refs_10_
  12.6 1.8 %pick.1 = (bf16[112,128]{1,0:T(8,128)(2,1)}, bf16[112,128]{1,0:T(8,128)(2,1)}, bf16[112,128]{1,0:T(8,128)(2,1)}, bf16[112,128]{1,0:T(8,128)(2,1)}) custom-call(s32[4,32]{1,0:T(4,128)} %bitcast.30, bf16[512,128]{1,0:T(8,128)(2,1)} %bitcast.22, s32[4,32]{1,0:T(4,128)} %bitcast.24, s32[4,1]{1,0:T(4,128)} %copy.14.count_ref.refs_7_.refs_10_, f32[4,32]{1,0:T(4,128)} %bitcast.27), custom_call_target="tpu_custom_call" | custom-call | tf_op jit(solution)/shard_map/pick/pallas_call | solution.py:295
  14.5 1.8 %collective-permute-start = (bf16[112,128]{1,0:T(8,128)(2,1)}, bf16[112,128]{1,0:T(8,128)(2,1)S(1)}, u32[]{:S(2)}, u32[]{:S(2)}) collective-permute-start(bf16[112,128]{1,0:T(8,128)(2,1)} %get-tuple-element.12), channel_id=1, source_target_pairs={{0,4},{4,8},{8,12},{12,0},{1,5},{5,9},{9,13},{13,1},{2,6},{6,10},{... | collective-permute-start | bytes 86024 | tf_op jit(solution)/shard_map/ppermute | solution.py:37
  16.3 4.1 %collective-permute-done.refs_1_.refs_4_ = bf16[112,128]{1,0:T(8,128)(2,1)S(1)} collective-permute-done((bf16[112,128]{1,0:T(8,128)(2,1)}, bf16[112,128]{1,0:T(8,128)(2,1)S(1)}, u32[]{:S(2)}, u32[]{:S(2)}) %collective-permute-start) | collective-permute-done | bytes 28704 | tf_op jit(solution)/shard_map/ppermute | solution.py:37
  20.4 1.0 %collective-permute-start.1 = (bf16[112,128]{1,0:T(8,128)(2,1)}, bf16[112,128]{1,0:T(8,128)(2,1)S(1)}, u32[]{:S(2)}, u32[]{:S(2)}) collective-permute-start(bf16[112,128]{1,0:T(8,128)(2,1)} %get-tuple-element.13), channel_id=1, source_target_pairs={{0,8},{4,12},{8,0},{12,4},{1,9},{5,13},{9,1},{13,5},{2,10},{6,14},... | collective-permute-start | bytes 86024 | tf_op jit(solution)/shard_map/ppermute | solution.py:37
  21.4 4.0 %collective-permute-done.1.refs_2_ = bf16[112,128]{1,0:T(8,128)(2,1)S(1)} collective-permute-done((bf16[112,128]{1,0:T(8,128)(2,1)}, bf16[112,128]{1,0:T(8,128)(2,1)S(1)}, u32[]{:S(2)}, u32[]{:S(2)}) %collective-permute-start.1) | collective-permute-done | bytes 28704 | tf_op jit(solution)/shard_map/ppermute | solution.py:37
  25.4 2.2 %collective-permute-start.2 = (bf16[112,128]{1,0:T(8,128)(2,1)}, bf16[112,128]{1,0:T(8,128)(2,1)S(1)}, u32[]{:S(2)}, u32[]{:S(2)}) collective-permute-start(bf16[112,128]{1,0:T(8,128)(2,1)} %get-tuple-element.14), channel_id=1, source_target_pairs={{0,12},{4,0},{8,4},{12,8},{1,13},{5,1},{9,5},{13,9},{2,14},{6,2},{... | collective-permute-start | bytes 86024 | tf_op jit(solution)/shard_map/ppermute | solution.py:37
  27.6 1.9 %collective-permute-done.2.refs_3_.refs_5_ = bf16[112,128]{1,0:T(8,128)(2,1)S(1)} collective-permute-done((bf16[112,128]{1,0:T(8,128)(2,1)}, bf16[112,128]{1,0:T(8,128)(2,1)S(1)}, u32[]{:S(2)}, u32[]{:S(2)}) %collective-permute-start.2) | collective-permute-done | bytes 28704 | tf_op jit(solution)/shard_map/ppermute | solution.py:37
  29.5 1.9 %collective-permute-start.3 = (bf16[128,512]{1,0:T(8,128)(2,1)S(1)}, bf16[128,512]{1,0:T(8,128)(2,1)S(1)}, u32[]{:S(2)}, u32[]{:S(2)}) collective-permute-start(bf16[128,512]{1,0:T(8,128)(2,1)S(1)} %copy-done.4), channel_id=1, source_target_pairs={{0,2},{2,0},{1,3},{3,1},{4,6},{6,4},{5,7},{7,5},{8,10},{10,8},{9,1... | collective-permute-start | bytes 393224 | tf_op jit(solution)/shard_map/ppermute | solution.py:37
  31.4 3.0 %collective-permute-done.3.refs_10_ = bf16[128,512]{1,0:T(8,128)(2,1)S(1)} collective-permute-done((bf16[128,512]{1,0:T(8,128)(2,1)S(1)}, bf16[128,512]{1,0:T(8,128)(2,1)S(1)}, u32[]{:S(2)}, u32[]{:S(2)}) %collective-permute-start.3) | collective-permute-done | bytes 131104 | tf_op jit(solution)/shard_map/ppermute | solution.py:37
  34.5 0.6 copy-done.5
  35.1 6.7 %attend.1 = (bf16[128,1024]{1,0:T(8,128)(2,1)}, bf16[128,1024]{1,0:T(8,128)(2,1)}) custom-call(bf16[112,128]{1,0:T(8,128)(2,1)} %get-tuple-element.11.refs_0_, bf16[112,128]{1,0:T(8,128)(2,1)} %copy-done.7, bf16[112,128]{1,0:T(8,128)(2,1)} %copy-done.9, bf16[112,128]{1,0:T(8,128)(2,1)} %copy-done.8, bf16[112,128]{1,0:T(8,128)(2,1)} %copy-done.7, ...), custom_call_target="tpu_custom_call" | custom-call | tf_op jit(solution)/shard_map/attend/pallas_call | solution.py:332
  41.9 2.0 %collective-permute-start.6 = (bf16[128,1024]{1,0:T(8,128)(2,1)}, bf16[128,1024]{1,0:T(8,128)(2,1)S(1)}, u32[]{:S(2)}, u32[]{:S(2)}) collective-permute-start(bf16[128,1024]{1,0:T(8,128)(2,1)} %get-tuple-element.15.refs_0_), channel_id=1, source_target_pairs={{0,2},{2,0},{1,3},{3,1},{4,6},{6,4},{5,7},{7,5},{8,10},{10,8},{9,1... | collective-permute-start | bytes 786440 | tf_op jit(solution)/shard_map/ppermute | solution.py:37
  44.0 4.5 %collective-permute-done.6.refs_1_ = bf16[128,1024]{1,0:T(8,128)(2,1)S(1)} collective-permute-done((bf16[128,1024]{1,0:T(8,128)(2,1)}, bf16[128,1024]{1,0:T(8,128)(2,1)S(1)}, u32[]{:S(2)}, u32[]{:S(2)}) %collective-permute-start.6) | collective-permute-done | bytes 262176 | tf_op jit(solution)/shard_map/ppermute | solution.py:37
  48.5 0.7 copy-done.3
  49.2 0.7 %copy-done = bf16[512,2048]{1,0:T(8,128)(2,1)} copy-done((bf16[512,2048]{1,0:T(8,128)(2,1)}, bf16[512,2048]{1,0:T(8,128)(2,1)S(1)}, u32[]{:S(2)}) %copy-start) | copy-done | bytes 2097176
  49.9 6.0 %finish.1 = bf16[8,32,128]{2,1,0:T(8,128)(2,1)} custom-call(bf16[128,1024]{1,0:T(8,128)(2,1)} %get-tuple-element.15.refs_0_, bf16[128,1024]{1,0:T(8,128)(2,1)} %copy-done.3, bf16[128,1024]{1,0:T(8,128)(2,1)} %get-tuple-element.16.refs_2_, bf16[512,2048]{1,0:T(8,128)(2,1)} %bitcast.17, bf16[512,2048]{1,0:T(8,128)(2,1)} %copy-done, f32[2048,128]{1,0:T(8,128)} %fold.1.refs_5_, ...), custom_call_target="tpu_custom_call" | custom-call | tf_op jit(solution)/shard_map/finish/pallas_call | solution.py:349
  56.0 6.2 %all-to-all-start = ((bf16[8,32,128]{2,1,0:T(8,128)(2,1)}), bf16[8,32,128]{2,1,0:T(8,128)(2,1)S(1)}, u32[]{:S(2)}, u32[]{:S(2)}) async-start(bf16[8,32,128]{2,1,0:T(8,128)(2,1)} %finish.1), calls=%async_computation | async-start | bytes 131072 | tf_op jit(solution)/shard_map/all_to_all | solution.py:361
  62.1 6.9 %all-to-all-done = bf16[8,32,128]{2,1,0:T(8,128)(2,1)S(1)} async-done(((bf16[8,32,128]{2,1,0:T(8,128)(2,1)}), bf16[8,32,128]{2,1,0:T(8,128)(2,1)S(1)}, u32[]{:S(2)}, u32[]{:S(2)}) %all-to-all-start) | async-done | bytes 65568 | tf_op jit(solution)/shard_map/all_to_all | solution.py:361
  69.0 1.8 %fusion.1 = bf16[1,512,128]{2,1,0:T(8,128)(2,1)} fusion(bf16[256,128]{1,0:T(8,128)(2,1)S(1)} %bitcast.23, s32[256]{0:T(256)S(1)} %eq.25, pred[512]{0:T(512)(128)(4,1)S(1)} %get-tuple-element.17, bf16[512,128]{1,0:T(8,128)(2,1)} %param.14, pred[512]{0:T(512)(128)(4,1)S(1)} %get-tuple-element.18, bf16[1,512,128]{2,1,0:T(8,128)(2,1)S(1)} %copy-done.6), kind=kOutput, calls=%fused_computation.2 | convolution fusion | flops 34078720 | bytes 460800 | tf_op jit(solution)/shard_map/dot_general | solution.py:24
  (33 shorter events, 1.2 us)
Async XLA Ops:
  0.0 12.0 %copy-start.12 = (s32[4,1]{0,1:T(1,128)S(1)}, s32[4,1]{0,1:T(1,128)}, u32[]{:S(2)}) copy-start(s32[4,1]{0,1:T(1,128)} %param.18) | copy-start | bytes 52
  0.0 29.5 %copy-start.4 = (bf16[128,512]{1,0:T(8,128)(2,1)S(1)}, bf16[128,512]{1,0:T(8,128)(2,1)}, u32[]{:S(2)}) copy-start(bf16[128,512]{1,0:T(8,128)(2,1)} %refs_9_.1) | copy-start | bytes 393220
  0.0 48.5 %collective-permute-start.7 = (bf16[512,2048]{1,0:T(8,128)(2,1)}, bf16[512,2048]{1,0:T(8,128)(2,1)S(1)}, u32[]{:S(2)}, u32[]{:S(2)}) collective-permute-start(bf16[512,2048]{1,0:T(8,128)(2,1)} %bitcast.16), channel_id=1, source_target_pairs={{0,1},{1,0},{2,3},{3,2},{4,5},{5,4},{6,7},{7,6},{8,9},{9,8},{10,11... | collective-permute-start | bytes 6291464 | tf_op jit(solution)/shard_map/ppermute | solution.py:37
  0.5 34.0 %collective-permute-start.4 = (bf16[3,512,512]{2,1,0:T(8,128)(2,1)}, bf16[3,512,512]{2,1,0:T(8,128)(2,1)}, u32[]{:S(2)}, u32[]{:S(2)}) collective-permute-start(bf16[3,512,512]{2,1,0:T(8,128)(2,1)} %bitcast.18), channel_id=1, source_target_pairs={{0,1},{1,0},{2,3},{3,2},{4,5},{5,4},{6,7},{7,6},{8,9},{9,8},{10,11... | collective-permute-start | bytes 4718600 | tf_op jit(solution)/shard_map/ppermute | solution.py:37
  0.6 6.9 %collective-permute-start.8 = (bf16[512,128]{1,0:T(8,128)(2,1)}, bf16[512,128]{1,0:T(8,128)(2,1)S(1)}, u32[]{:S(2)}, u32[]{:S(2)}) collective-permute-start(bf16[512,128]{1,0:T(8,128)(2,1)} %refs_7_.2), channel_id=1, source_target_pairs={{0,2},{2,0},{1,3},{3,1},{4,6},{6,4},{5,7},{7,5},{8,10},{10,8},{9,1... | collective-permute-start | bytes 393224 | tf_op jit(solution)/shard_map/ppermute | solution.py:37
  7.4 0.6 copy-start.2
  11.5 32.5 %collective-permute-start.9 = (f32[2048,128]{1,0:T(8,128)}, f32[2048,128]{1,0:T(8,128)S(1)}, u32[]{:S(2)}, u32[]{:S(2)}) collective-permute-start(f32[2048,128]{1,0:T(8,128)} %fold.1.refs_5_), channel_id=1, source_target_pairs={{0,1},{1,0},{2,3},{3,2},{4,5},{5,4},{6,7},{7,6},{8,9},{9,8},{10,11... | collective-permute-start | bytes 3145736 | tf_op jit(solution)/shard_map/ppermute | solution.py:37
  11.5 23.0 %collective-permute-start.5 = (bf16[512,512]{1,0:T(8,128)(2,1)}, bf16[512,512]{1,0:T(8,128)(2,1)}, u32[]{:S(2)}, u32[]{:S(2)}) collective-permute-start(bf16[512,512]{1,0:T(8,128)(2,1)} %bitcast.20), channel_id=1, source_target_pairs={{0,1},{1,0},{2,3},{3,2},{4,5},{5,4},{6,7},{7,6},{8,9},{9,8},{10,11... | collective-permute-start | bytes 1572872 | tf_op jit(solution)/shard_map/ppermute | solution.py:37
  14.5 5.9 %collective-permute-start = (bf16[112,128]{1,0:T(8,128)(2,1)}, bf16[112,128]{1,0:T(8,128)(2,1)S(1)}, u32[]{:S(2)}, u32[]{:S(2)}) collective-permute-start(bf16[112,128]{1,0:T(8,128)(2,1)} %get-tuple-element.12), channel_id=1, source_target_pairs={{0,4},{4,8},{8,12},{12,0},{1,5},{5,9},{9,13},{13,1},{2,6},{6,10},{... | collective-permute-start | bytes 86024 | tf_op jit(solution)/shard_map/ppermute | solution.py:37
  20.4 14.1 %copy-start.7 = (bf16[112,128]{1,0:T(8,128)(2,1)}, bf16[112,128]{1,0:T(8,128)(2,1)S(1)}, u32[]{:S(2)}) copy-start(bf16[112,128]{1,0:T(8,128)(2,1)S(1)} %collective-permute-done.refs_1_.refs_4_) | copy-start | bytes 86020
  20.4 5.0 %collective-permute-start.1 = (bf16[112,128]{1,0:T(8,128)(2,1)}, bf16[112,128]{1,0:T(8,128)(2,1)S(1)}, u32[]{:S(2)}, u32[]{:S(2)}) collective-permute-start(bf16[112,128]{1,0:T(8,128)(2,1)} %get-tuple-element.13), channel_id=1, source_target_pairs={{0,8},{4,12},{8,0},{12,4},{1,9},{5,13},{9,1},{13,5},{2,10},{6,14},... | collective-permute-start | bytes 86024 | tf_op jit(solution)/shard_map/ppermute | solution.py:37
  25.4 9.1 %copy-start.9 = (bf16[112,128]{1,0:T(8,128)(2,1)}, bf16[112,128]{1,0:T(8,128)(2,1)S(1)}, u32[]{:S(2)}) copy-start(bf16[112,128]{1,0:T(8,128)(2,1)S(1)} %collective-permute-done.1.refs_2_) | copy-start | bytes 86020
  25.4 4.1 %collective-permute-start.2 = (bf16[112,128]{1,0:T(8,128)(2,1)}, bf16[112,128]{1,0:T(8,128)(2,1)S(1)}, u32[]{:S(2)}, u32[]{:S(2)}) collective-permute-start(bf16[112,128]{1,0:T(8,128)(2,1)} %get-tuple-element.14), channel_id=1, source_target_pairs={{0,12},{4,0},{8,4},{12,8},{1,13},{5,1},{9,5},{13,9},{2,14},{6,2},{... | collective-permute-start | bytes 86024 | tf_op jit(solution)/shard_map/ppermute | solution.py:37
  29.5 5.0 %copy-start.8 = (bf16[112,128]{1,0:T(8,128)(2,1)}, bf16[112,128]{1,0:T(8,128)(2,1)S(1)}, u32[]{:S(2)}) copy-start(bf16[112,128]{1,0:T(8,128)(2,1)S(1)} %collective-permute-done.2.refs_3_.refs_5_) | copy-start | bytes 86020
  29.5 5.0 %collective-permute-start.3 = (bf16[128,512]{1,0:T(8,128)(2,1)S(1)}, bf16[128,512]{1,0:T(8,128)(2,1)S(1)}, u32[]{:S(2)}, u32[]{:S(2)}) collective-permute-start(bf16[128,512]{1,0:T(8,128)(2,1)S(1)} %copy-done.4), channel_id=1, source_target_pairs={{0,2},{2,0},{1,3},{3,1},{4,6},{6,4},{5,7},{7,5},{8,10},{10,8},{9,1... | collective-permute-start | bytes 393224 | tf_op jit(solution)/shard_map/ppermute | solution.py:37
  34.5 0.7 copy-start.5
  35.1 8.8 %copy-start.10 = (s32[1,4,32]{2,1,0:T(4,128)S(1)}, s32[1,4,32]{2,1,0:T(4,128)}, u32[]{:S(2)}) copy-start(s32[1,4,32]{2,1,0:T(4,128)} %param.16) | copy-start | bytes 1540
  41.9 6.6 %collective-permute-start.6 = (bf16[128,1024]{1,0:T(8,128)(2,1)}, bf16[128,1024]{1,0:T(8,128)(2,1)S(1)}, u32[]{:S(2)}, u32[]{:S(2)}) collective-permute-start(bf16[128,1024]{1,0:T(8,128)(2,1)} %get-tuple-element.15.refs_0_), channel_id=1, source_target_pairs={{0,2},{2,0},{1,3},{3,1},{4,6},{6,4},{5,7},{7,5},{8,10},{10,8},{9,1... | collective-permute-start | bytes 786440 | tf_op jit(solution)/shard_map/ppermute | solution.py:37
  44.0 4.6 %copy-start.1 = (f32[2048,128]{1,0:T(8,128)}, f32[2048,128]{1,0:T(8,128)S(1)}, u32[]{:S(2)}) copy-start(f32[2048,128]{1,0:T(8,128)S(1)} %collective-permute-done.9.refs_6_) | copy-start | bytes 3145732
  48.5 0.7 copy-start.3
  48.5 1.4 %copy-start = (bf16[512,2048]{1,0:T(8,128)(2,1)}, bf16[512,2048]{1,0:T(8,128)(2,1)S(1)}, u32[]{:S(2)}) copy-start(bf16[512,2048]{1,0:T(8,128)(2,1)S(1)} %collective-permute-done.7.refs_4_) | copy-start | bytes 6291460
  49.9 12.2 %copy-start.11 = (s32[512]{0:T(512)S(1)}, s32[512]{0:T(512)}, u32[]{:S(2)}) copy-start(s32[512]{0:T(512)} %param.15) | copy-start | bytes 6148
  49.9 19.1 %copy-start.6 = (bf16[1,512,128]{2,1,0:T(8,128)(2,1)S(1)}, bf16[1,512,128]{2,1,0:T(8,128)(2,1)}, u32[]{:S(2)}) copy-start(bf16[1,512,128]{2,1,0:T(8,128)(2,1)} %param.13) | copy-start | bytes 393220
  56.0 13.1 %all-to-all-start = ((bf16[8,32,128]{2,1,0:T(8,128)(2,1)}), bf16[8,32,128]{2,1,0:T(8,128)(2,1)S(1)}, u32[]{:S(2)}, u32[]{:S(2)}) async-start(bf16[8,32,128]{2,1,0:T(8,128)(2,1)} %finish.1), calls=%async_computation | async-start | bytes 131072 | tf_op jit(solution)/shard_map/all_to_all | solution.py:361
